TPU v7x, 32 devices: a whole 2x2x4 slice. The times are simulated.
32 devices in a mesh: lat: 4 (over y, core), lon: 8 (over z, x).
Axes of the slice: x: 2, y: 2, z: 4, core: 2. Of those that a mesh axis runs over, the one named last changes fastest.
Arguments:
- inputs: bfloat16 [8, 24, 96, 192], P(None, 'lat', 'lon'), may hold values from -6 to 6
- cotangent: bfloat16 [8, 24, 96, 192], P(None, 'lat', 'lon'), may hold values from -6 to 6
- qkv_weight: bfloat16 [192, 576], P(None, 'lon'), may hold values from -0.4375 to 0.4375
- proj_weight: bfloat16 [192, 192], P(None, 'lon'), may hold values from -0.4375 to 0.4375
- up_weight: bfloat16 [192, 768], P(None, 'lon'), may hold values from -0.4375 to 0.4375
- down_weight: bfloat16 [768, 192], P(None, 'lon'), may hold values from -0.21875 to 0.21875
- norm_gains: bfloat16 [2, 192], P(None, 'lon'), may hold values from 0.099609375 to 1.8984375
- bias_table: bfloat16 [16, 6, 20736], P(None, None, 'lon'), may hold values from -4 to 304
- type_of: int32 [4, 4], replicated, may hold values from 0 to 15
- region: int32 [8, 24], P(None, 'lat'), may hold values from 0 to 2
Outputs:
- grad_input: bfloat16 [8, 24, 96, 192], P(None, 'lat', 'lon')
- grad_qkv: float32 [192, 576], P(None, 'lon')
- grad_proj: float32 [192, 192], P(None, 'lon')
- grad_up: float32 [192, 768], P(None, 'lon')
- grad_down: float32 [768, 192], P(None, 'lon')
- grad_gains: float32 [2, 192], P(None, 'lon')
- grad_table: float32 [16, 6, 20736], P(None, None, 'lon')
Inputs may be any that keep to these rules, and one draw needn't show every extreme that they name: `type_of`: types may repeat and some may be absent. Attention joins only tokens of a window with equal region ids.
All inputs are finite; a program needn't handle non-finite values.
Results may differ from a plain program's by a relative error of at most 0.015.
Values may be sent and summed in bfloat16 or wider, within the bound.
A program may use at most 64 MiB of HBM per device.

v0:
```python
import math

import jax
import jax.numpy as jnp
from jax import lax
from jax.sharding import PartitionSpec as P

WPL = 2
WLAT = 6
WLON = 12
WIN = 144


def passed_along(block, axis, distance):
    devices = range(lax.axis_size(axis))
    route = [((i - distance) % len(devices), i) for i in devices]
    return lax.ppermute(block, axis, route)


def layer_norm(values):
    row_mean = jnp.mean(values, axis=-1, keepdims=True)
    centred = values - row_mean
    variance = jnp.mean(centred * centred, axis=-1, keepdims=True)
    inv_std = lax.rsqrt(variance + 1e-05)
    return (centred * inv_std, inv_std)


def norm_back(d_normed, normed, inv_std):
    return inv_std * (
        d_normed
        - jnp.mean(d_normed, axis=-1, keepdims=True)
        - normed * jnp.mean(d_normed * normed, axis=-1, keepdims=True)
    )


def gelu_pair(pre_act):
    cumul = 0.5 * (1.0 + lax.erf(pre_act * 0.7071067811865476))
    density = jnp.exp(-0.5 * pre_act * pre_act) * 0.3989422804014327
    return (pre_act * cumul, cumul + pre_act * density)


def to_windows(column, level_windows, row_windows):
    features = column.shape[-1]
    shaped = column.reshape(level_windows, WPL, row_windows, WLAT, WLON, features)
    return shaped.transpose(0, 2, 1, 3, 4, 5).reshape(level_windows * row_windows * WIN, features)


def from_windows(flat, level_windows, row_windows):
    features = flat.shape[-1]
    shaped = flat.reshape(level_windows, row_windows, WPL, WLAT, WLON, features)
    return shaped.transpose(0, 2, 1, 3, 4, 5).reshape(
        level_windows * WPL, row_windows * WLAT, WLON, features
    )


def region_mask(region_rows, level_windows, row_windows):
    labels = region_rows.reshape(level_windows, WPL, row_windows, WLAT).transpose(0, 2, 1, 3)
    labels = jnp.broadcast_to(labels[..., None], (level_windows, row_windows, WPL, WLAT, WLON))
    labels = labels.reshape(level_windows, row_windows, WIN)
    return labels[..., :, None] == labels[..., None, :]


def roll_block(stacked, forward):
    level_shift = WPL // 2
    stacked = jnp.roll(stacked, -level_shift if forward else level_shift, axis=1)
    row_half = WLAT // 2
    rim_rows = stacked[:, :, :row_half] if forward else stacked[:, :, -row_half:]
    arrived = passed_along(rim_rows, "lat", -1 if forward else 1)
    if forward:
        stacked = jnp.concatenate([stacked[:, :, row_half:], arrived], axis=2)
    else:
        stacked = jnp.concatenate([arrived, stacked[:, :, :-row_half]], axis=2)
    col_half = WLON // 2
    rim_cols = stacked[:, :, :, :col_half] if forward else stacked[:, :, :, -col_half:]
    landed = passed_along(rim_cols, "lon", -1 if forward else 1)
    if forward:
        stacked = jnp.concatenate([stacked[:, :, :, col_half:], landed], axis=3)
    else:
        stacked = jnp.concatenate([landed, stacked[:, :, :, :-col_half]], axis=3)
    return stacked


def column_grads(column, cot_column, weights, bias_pos, same_region):
    qkv_full, proj_full, up_full, down_full, gains_full = weights
    f32 = jnp.float32
    bf16 = jnp.bfloat16
    level_windows = column.shape[0] // WPL
    row_windows = column.shape[1] // WLAT
    features = column.shape[-1]
    head_count = bias_pos.shape[2]
    head_size = features // head_count
    factor = 1.0 / math.sqrt(head_size)
    gain_one = gains_full[0].astype(f32)
    gain_two = gains_full[1].astype(f32)
    window_cells = to_windows(column, level_windows, row_windows).astype(f32)
    normed_one, inv_one = layer_norm(window_cells)
    scaled_one = (normed_one * gain_one).astype(bf16)
    packed = jnp.dot(scaled_one, qkv_full, preferred_element_type=f32).astype(bf16)
    packed = packed.reshape(level_windows, row_windows, WIN, 3, head_count, head_size)
    queries = packed[:, :, :, 0]
    key_rows = packed[:, :, :, 1]
    value_rows = packed[:, :, :, 2]
    scores = (
        jnp.einsum("abthd,abshd->abhts", queries, key_rows, preferred_element_type=f32) * factor
    )
    scores = scores + bias_pos.astype(f32)
    scores = jnp.where(same_region[:, :, None], scores, -jnp.inf)
    peak_score = jnp.max(scores, axis=-1, keepdims=True)
    raised = jnp.exp(scores - peak_score)
    attn_probs = raised / jnp.sum(raised, axis=-1, keepdims=True)
    probs_b = attn_probs.astype(bf16)
    attended = jnp.einsum("abhts,abshd->abthd", probs_b, value_rows, preferred_element_type=f32)
    attended = attended.astype(bf16).reshape(-1, features)
    middle = window_cells + jnp.dot(attended, proj_full, preferred_element_type=f32)
    normed_two, inv_two = layer_norm(middle)
    scaled_two = (normed_two * gain_two).astype(bf16)
    pre_act = jnp.dot(scaled_two, up_full, preferred_element_type=f32)
    activated, gelu_slope = gelu_pair(pre_act)
    hidden_b = activated.astype(bf16)
    cot_rows = to_windows(cot_column, level_windows, row_windows)
    grad_down = jnp.dot(hidden_b.T, cot_rows, preferred_element_type=f32)
    d_hidden = (jnp.dot(cot_rows, down_full.T, preferred_element_type=f32) * gelu_slope).astype(
        bf16
    )
    grad_up = jnp.dot(scaled_two.T, d_hidden, preferred_element_type=f32)
    d_htwo = jnp.dot(d_hidden, up_full.T, preferred_element_type=f32)
    gain_grad_two = jnp.sum(d_htwo * normed_two, axis=0)
    d_middle = cot_rows.astype(f32) + norm_back(d_htwo * gain_two, normed_two, inv_two)
    d_middle_b = d_middle.astype(bf16)
    grad_proj = jnp.dot(attended.T, d_middle_b, preferred_element_type=f32)
    d_att = jnp.dot(d_middle_b, proj_full.T, preferred_element_type=f32).astype(bf16)
    d_att = d_att.reshape(level_windows, row_windows, WIN, head_count, head_size)
    d_prob = jnp.einsum("abthd,abshd->abhts", d_att, value_rows, preferred_element_type=f32)
    d_values = jnp.einsum("abhts,abthd->abshd", probs_b, d_att, preferred_element_type=f32)
    d_score = attn_probs * (d_prob - jnp.sum(attn_probs * d_prob, axis=-1, keepdims=True))
    d_score_b = d_score.astype(bf16)
    d_queries = (
        jnp.einsum("abhts,abshd->abthd", d_score_b, key_rows, preferred_element_type=f32) * factor
    )
    d_keys = (
        jnp.einsum("abhts,abthd->abshd", d_score_b, queries, preferred_element_type=f32) * factor
    )
    d_packed = (
        jnp.stack([d_queries, d_keys, d_values], axis=3).astype(bf16).reshape(-1, 3 * features)
    )
    grad_qkv = jnp.dot(scaled_one.T, d_packed, preferred_element_type=f32)
    d_hone = jnp.dot(d_packed, qkv_full.T, preferred_element_type=f32)
    gain_grad_one = jnp.sum(d_hone * normed_one, axis=0)
    d_cells = d_middle + norm_back(d_hone * gain_one, normed_one, inv_one)
    d_column = from_windows(d_cells.astype(bf16), level_windows, row_windows)
    param_grads = (
        grad_qkv,
        grad_proj,
        grad_up,
        grad_down,
        jnp.stack([gain_grad_one, gain_grad_two]),
    )
    table_grad = d_score.reshape(level_windows * row_windows, head_count, WIN * WIN)
    return (d_column, param_grads, table_grad)


def shards(
    inputs,
    cotangent,
    qkv_weight,
    proj_weight,
    up_weight,
    down_weight,
    norm_gains,
    bias_table,
    type_of,
    region,
):
    level_windows = inputs.shape[0] // WPL
    row_windows = inputs.shape[1] // WLAT
    lon_windows = inputs.shape[2] // WLON
    features = inputs.shape[3]
    type_count = bias_table.shape[0]
    head_count = bias_table.shape[1]
    positions = level_windows * row_windows
    lat_index = lax.axis_index("lat")
    type_rows = lax.dynamic_slice(
        type_of, (jnp.int32(0), lat_index * row_windows), (level_windows, row_windows)
    ).reshape(-1)
    onehot = type_rows[:, None] == jnp.arange(type_count, dtype=jnp.int32)[None, :]
    select_half = onehot.astype(jnp.bfloat16)
    select_full = onehot.astype(jnp.float32)
    table_part = bias_table.reshape(type_count * head_count, -1)
    qkv_full, proj_full, up_full, down_full, gains_full, table_full = (
        lax.all_gather(qkv_weight, "lon", axis=1, tiled=True),
        lax.all_gather(proj_weight, "lon", axis=1, tiled=True),
        lax.all_gather(up_weight, "lon", axis=1, tiled=True),
        lax.all_gather(down_weight, "lon", axis=1, tiled=True),
        lax.all_gather(norm_gains, "lon", axis=1, tiled=True),
        lax.all_gather(table_part, "lon", axis=1, tiled=True),
    )
    chosen_rows = jnp.dot(
        select_half, table_full.reshape(type_count, -1), preferred_element_type=jnp.float32
    )
    bias_pos = chosen_rows.astype(jnp.bfloat16).reshape(
        level_windows, row_windows, head_count, WIN, WIN
    )
    same_region = region_mask(region, level_windows, row_windows)
    shifted = roll_block(jnp.stack([inputs, cotangent]), True)
    columns = shifted.reshape(2, inputs.shape[0], inputs.shape[1], lon_windows, WLON, features)
    columns = columns.transpose(3, 0, 1, 2, 4, 5)
    weights = (qkv_full, proj_full, up_full, down_full, gains_full)

    def advance(totals, column_pair):
        d_column, param_grads, table_grad = column_grads(
            column_pair[0], column_pair[1], weights, bias_pos, same_region
        )
        return (jax.tree.map(jnp.add, totals, (param_grads, table_grad)), d_column)

    initial = (
        tuple((jnp.zeros(member.shape, jnp.float32) for member in weights)),
        jnp.zeros((positions, head_count, WIN * WIN), jnp.float32),
    )
    totals, d_columns = lax.scan(advance, initial, columns)
    d_shifted = d_columns.transpose(1, 2, 0, 3, 4).reshape(inputs.shape)
    grad_input = roll_block(d_shifted[None], False)[0]
    param_grads, table_sum = totals
    table_member = jnp.dot(
        select_full.T, table_sum.reshape(positions, -1), precision=lax.Precision.HIGHEST
    ).reshape(type_count * head_count, -1)
    summed = (
        lax.psum_scatter(param_grads[0], "lon", scatter_dimension=1, tiled=True),
        lax.psum_scatter(param_grads[1], "lon", scatter_dimension=1, tiled=True),
        lax.psum_scatter(param_grads[2], "lon", scatter_dimension=1, tiled=True),
        lax.psum_scatter(param_grads[3], "lon", scatter_dimension=1, tiled=True),
        lax.psum_scatter(param_grads[4], "lon", scatter_dimension=1, tiled=True),
        lax.psum_scatter(table_member, "lon", scatter_dimension=1, tiled=True),
    )
    table_shard = summed[5]
    lat_sums = (
        lax.psum(summed[0].astype(jnp.bfloat16), "lat").astype(jnp.float32),
        lax.psum(summed[1].astype(jnp.bfloat16), "lat").astype(jnp.float32),
        lax.psum(summed[2].astype(jnp.bfloat16), "lat").astype(jnp.float32),
        lax.psum(summed[3].astype(jnp.bfloat16), "lat").astype(jnp.float32),
        lax.psum(summed[4].astype(jnp.bfloat16), "lat").astype(jnp.float32),
        lax.psum(table_shard.astype(jnp.bfloat16), "lat").astype(jnp.float32),
    )
    token_count = (
        inputs.shape[0]
        * inputs.shape[1]
        * inputs.shape[2]
        * lax.axis_size("lat")
        * lax.axis_size("lon")
    )
    factor = 1.0 / math.sqrt(token_count)
    return (
        grad_input,
        lat_sums[0] * factor,
        lat_sums[1] * factor,
        lat_sums[2] * factor,
        lat_sums[3] * factor,
        lat_sums[4] * factor,
        lat_sums[5].reshape(type_count, head_count, -1),
    )


def solution(mesh):
    return jax.shard_map(
        shards,
        mesh=mesh,
        in_specs=(
            P(None, "lat", "lon", None),
            P(None, "lat", "lon", None),
            P(None, "lon"),
            P(None, "lon"),
            P(None, "lon"),
            P(None, "lon"),
            P(None, "lon"),
            P(None, None, "lon"),
            P(),
            P(None, "lat"),
        ),
        out_specs=(
            P(None, "lat", "lon", None),
            P(None, "lon"),
            P(None, "lon"),
            P(None, "lon"),
            P(None, "lon"),
            P(None, "lon"),
            P(None, None, "lon"),
        ),
        check_vma=False,
    )
```

profile of v0, /device:TPU:0, one launch (start us, length us, event | category | flops | bytes accessed | tf_op | source)
XLA Modules:
  0.0 769.3 jit_solution(3788495706236604130)
XLA Ops:
  13.8 21.2 %all-gather = bf16[8,24,2]{1,2,0:T(2,128)(2,1)S(1)} all-gather(bf16[1,24,2]{1,2,0:T(2,128)(2,1)S(1)} %bitcast.117), channel_id=1, replica_groups=mesh['lat'=4,'lon'=8] {'lon'}, dimensions={0}, use_global_device_ids=true | all-gather | bytes 864 | tf_op jit(solution)/shard_map/all_gather | solution.py:194
  35.6 33.6 %all_gather.21 = bf16[192,192]{0,1:T(8,128)(2,1)} all-gather(bf16[192,24]{0,1:T(8,128)(2,1)S(1)} %copy-done.32), channel_id=1, replica_groups=mesh['lat'=4,'lon'=8] {'lon'}, dimensions={1}, use_global_device_ids=true | all-gather | bytes 82944 | tf_op jit(solution)/shard_map/all_gather | solution.py:191
  69.2 31.9 %all_gather.19 = bf16[192,576]{0,1:T(8,128)(2,1)S(1)} all-gather(bf16[192,72]{0,1:T(8,128)(2,1)S(1)} %copy-done.27), channel_id=1, replica_groups=mesh['lat'=4,'lon'=8] {'lon'}, dimensions={1}, use_global_device_ids=true | all-gather | bytes 248832 | tf_op jit(solution)/shard_map/all_gather | solution.py:190
  101.1 32.9 %all_gather.22 = bf16[768,192]{0,1:T(8,128)(2,1)} all-gather(bf16[768,24]{0,1:T(8,128)(2,1)S(1)} %copy-done.28), channel_id=1, replica_groups=mesh['lat'=4,'lon'=8] {'lon'}, dimensions={1}, use_global_device_ids=true | all-gather | bytes 331776 | tf_op jit(solution)/shard_map/all_gather | solution.py:193
  134.0 33.3 %all_gather.23 = bf16[192,768]{0,1:T(8,128)(2,1)} all-gather(bf16[192,96]{0,1:T(8,128)(2,1)S(1)} %copy.75), channel_id=1, replica_groups=mesh['lat'=4,'lon'=8] {'lon'}, dimensions={1}, use_global_device_ids=true | all-gather | bytes 331776 | tf_op jit(solution)/shard_map/all_gather | solution.py:192
  169.7 5.7 collective-permute-done.1
  182.2 5.3 copy.70
  187.6 7.1 reshape.310
  194.7 7.4 reshape.296
  202.1 4.2 fusion.1
  206.2 4.7 reshape.305
  211.0 3.5 copy.71
  214.5 3.0 add_select_fusion
  217.6 3.0 fusion.37
  241.9 3.1 multiply_reduce_fusion
  252.3 3.3 convert_element_type.168
  258.2 2.8 convolution_bitcast_fusion
  261.1 2.9 fusion.11
  265.3 3.4 copy.84
  268.7 4.8 reshape.299
  274.9 20.3 %all-reduce = bf16[2,192]{1,0:T(2,128)(2,1)S(1)} all-reduce(f32[2,192]{1,0:T(2,128)S(1)} %pad_maximum_fusion.4), channel_id=6, replica_groups=mesh['lat'=4,'lon'=8] {'lon'}, use_global_device_ids=true, to_apply=%region_21.22.clone | all-reduce | flops 384 | bytes 2304
  295.7 14.1 %reduce-scatter.13.cloned.1.call-done = f32[192,24]{0,1:T(8,128)} async-done(((f32[192,192]{0,1:T(8,128)}), f32[192,24]{0,1:T(8,128)}) %reduce-scatter.13.cloned.1.call-update) | async-done | bytes 18448 | tf_op jit(solution)/shard_map/reduce_scatter | solution.py:228
  311.1 63.6 %reduce-scatter.11.cloned.1.call-done = f32[192,72]{0,1:T(8,128)} async-done(((f32[192,576]{0,1:T(8,128)}), f32[192,72]{0,1:T(8,128)}) %reduce-scatter.11.cloned.1.call-update) | async-done | bytes 55312 | tf_op jit(solution)/shard_map/reduce_scatter | solution.py:227
  376.3 64.0 %reduce-scatter.17.cloned.1.call-done = f32[96,192]{1,0:T(8,128)} async-done(((f32[768,192]{1,0:T(8,128)}), f32[96,192]{1,0:T(8,128)}) %reduce-scatter.17.cloned.1.call-update) | async-done | bytes 73744
  441.9 63.8 %reduce-scatter.15.cloned.1.call-done = f32[768,24]{0,1:T(8,128)} async-done(((f32[768,192]{0,1:T(8,128)}), f32[768,24]{0,1:T(8,128)}) %reduce-scatter.15.cloned.1.call-update) | async-done | bytes 73744 | tf_op jit(solution)/shard_map/reduce_scatter | solution.py:230
  507.3 5.8 fusion.30
  513.1 6.2 reshape.300
  519.2 9.5 %copy.95 = f32[96,20736]{0,1:T(8,128)} copy(f32[96,20736]{1,0:T(8,128)} %reshape.300) | data formatting | bytes 15925248
  530.6 5.7 collective-permute-done.2
  537.8 7.1 collective-permute-done.3
  550.1 173.8 %reduce-scatter.19.cloned.1.call-done = f32[2592,96]{1,0:T(8,128)} async-done(((f32[20736,96]{1,0:T(8,128)}), f32[2592,96]{1,0:T(8,128)}) %reduce-scatter.19.cloned.1.call-update) | async-done | bytes 995344
  727.9 32.3 %all-reduce.5.cloned.1.call-done = bf16[16,6,2592]{2,1,0:T(8,128)(2,1)} async-done(((bf16[16,6,2592]{2,1,0:T(8,128)(2,1)}), bf16[16,6,2592]{2,1,0:T(8,128)(2,1)}) %all-reduce.5.cloned.1.call-update) | async-done | bytes 497680 | tf_op jit(solution)/shard_map/psum | solution.py:241
  (189 shorter events, 70.0 us)
Async XLA Ops:
  7.2 28.2 %copy-start = (s32[4,4]{1,0:T(4,128)S(1)}, s32[4,4]{1,0:T(4,128)}, u32[]{:S(2)}) copy-start(s32[4,4]{1,0:T(4,128)} %param.18) | copy-start | bytes 196
  7.2 6.6 copy-start.37
  7.2 27.8 %copy-start.36 = (s32[8,6]{1,0:T(8,128)S(1)}, s32[8,6]{1,0:T(8,128)}, u32[]{:S(2)}) copy-start(s32[8,6]{1,0:T(8,128)} %param.19) | copy-start | bytes 580
  7.2 28.0 %copy-start.25 = (bf16[192,96]{1,0:T(8,128)(2,1)S(1)}, bf16[192,96]{1,0:T(8,128)(2,1)}, u32[]{:S(2)}) copy-start(bf16[192,96]{1,0:T(8,128)(2,1)} %param.14) | copy-start | bytes 110596
  7.2 28.3 %copy-start.32 = (bf16[192,24]{0,1:T(8,128)(2,1)S(1)}, bf16[192,24]{0,1:T(8,128)(2,1)}, u32[]{:S(2)}) copy-start(bf16[192,24]{0,1:T(8,128)(2,1)} %param.13) | copy-start | bytes 27652
  7.2 61.9 %copy-start.27 = (bf16[192,72]{0,1:T(8,128)(2,1)S(1)}, bf16[192,72]{0,1:T(8,128)(2,1)}, u32[]{:S(2)}) copy-start(bf16[192,72]{0,1:T(8,128)(2,1)} %param.12) | copy-start | bytes 82948
  7.3 175.0 %all-gather.4.cloned.1.call-start = ((), (), s32[]{:S(2)}) async-start(), calls=%async_computation.9 | async-start | bytes 4644864 | tf_op jit(solution)/shard_map/all_gather | solution.py:195
  8.5 92.5 %copy-start.28 = (bf16[768,24]{0,1:T(8,128)(2,1)S(1)}, bf16[768,24]{0,1:T(8,128)(2,1)}, u32[]{:S(2)}) copy-start(bf16[768,24]{0,1:T(8,128)(2,1)} %param.15) | copy-start | bytes 110596
  9.7 300.1 %reduce-scatter.13.cloned.1.call-start = ((), (), s32[]{:S(2)}) async-start(), calls=%async_computation.6 | async-start | bytes 221184 | tf_op jit(solution)/shard_map/reduce_scatter | solution.py:228
  11.3 156.8 %collective-permute-start = (bf16[2,8,3,12,192]{4,1,3,2,0:T(8,128)(2,1)S(1)}, bf16[2,8,3,12,192]{4,1,3,2,0:T(8,128)(2,1)S(1)}, u32[]{:S(2)}, u32[]{:S(2)}) collective-permute-start(bf16[2,8,3,12,192]{4,1,3,2,0:T(8,128)(2,1)S(1)} %get-tuple-element.87), channel_id=1, source_target_pairs={{8,0},{16,8},{24,16},{0,24},{9,1},{17,9},{25,17},{1,25},{10,2},{18... | collective-permute-start | bytes 663560 | tf_op jit(solution)/shard_map/ppermute | solution.py:17
  35.6 166.5 %copy-start.33 = (s32[4]{0:T(128)}, s32[4]{0:T(128)S(1)}, u32[]{:S(2)}) copy-start(s32[4]{0:T(128)S(1)} %dynamic-slice_reduce_fusion) | copy-start | bytes 52
  101.1 78.0 %copy-start.19 = (bf16[192,576]{0,1:T(8,128)(2,1)}, bf16[192,576]{0,1:T(8,128)(2,1)S(1)}, u32[]{:S(2)}) copy-start(bf16[192,576]{0,1:T(8,128)(2,1)S(1)} %all_gather.19) | copy-start | bytes 663556
  168.2 7.2 collective-permute-start.1
  169.7 9.4 %copy-start.30 = (f32[1,192]{1,0:T(1,128)}, f32[1,192]{1,0:T(1,128)S(1)}, u32[]{:S(2)}) copy-start(f32[1,192]{1,0:T(1,128)S(1)} %get-tuple-element.92) | copy-start | bytes 2308
  228.9 4.3 copy-start.2
  248.8 126.0 %reduce-scatter.11.cloned.1.call-start = ((), (), s32[]{:S(2)}) async-start(), calls=%async_computation.5 | async-start | bytes 663552 | tf_op jit(solution)/shard_map/reduce_scatter | solution.py:227
  258.1 182.1 %reduce-scatter.17.cloned.1.call-start = ((), (), s32[]{:S(2)}) async-start(), calls=%async_computation.10 | async-start | bytes 884736
  261.0 244.7 %reduce-scatter.15.cloned.1.call-start = ((), (), s32[]{:S(2)}) async-start(), calls=%async_computation.7 | async-start | bytes 663552 | tf_op jit(solution)/shard_map/reduce_scatter | solution.py:230
  264.0 281.9 %all-reduce.7.cloned.1.call-start = ((), (), s32[]{:S(2)}) async-start(), calls=%async_computation.12 | async-start | bytes 271360 | tf_op jit(solution)/shard_map/psum | solution.py:236
  268.7 4.9 copy-start.7
  268.7 4.9 copy-start.13
  268.7 4.9 copy-start.20
  268.7 4.9 copy-start.31
  268.7 6.2 copy-start.35
  268.7 238.5 %copy-start.34 = (s32[4]{0:T(128)S(1)}, s32[4]{0:T(128)}, u32[]{:S(2)}) copy-start(s32[4]{0:T(128)} %copy-done.33) | copy-start | bytes 52
  507.2 216.7 %reduce-scatter.19.cloned.1.call-start = ((), (), s32[]{:S(2)}) async-start(), calls=%async_computation.11 | async-start | bytes 11943936
  528.8 231.3 %all-reduce.5.cloned.1.call-start = ((), (), s32[]{:S(2)}) async-start(), calls=%async_computation.8 | async-start | bytes 1376256 | tf_op jit(solution)/shard_map/psum | solution.py:241
  530.5 5.8 collective-permute-start.2
  536.5 8.4 %collective-permute-start.3 = (bf16[1,8,6,6,192]{4,3,2,1,0:T(8,128)(2,1)S(1)}, bf16[1,8,6,6,192]{4,3,2,1,0:T(8,128)(2,1)S(1)}, u32[]{:S(2)}, u32[]{:S(2)}) collective-permute-start(bf16[1,8,6,6,192]{4,3,2,1,0:T(8,128)(2,1)S(1)} %get-tuple-element.89), channel_id=1, source_target_pairs={{7,0},{0,1},{1,2},{2,3},{3,4},{4,5},{5,6},{6,7},{15,8},{8,9},{9,10... | collective-permute-start | bytes 331784 | tf_op jit(solution)/shard_map/ppermute | solution.py:17
  544.9 217.3 %copy-start.1 = (s32[4,4]{1,0:T(4,128)S(1)}, s32[4,4]{1,0:T(4,128)}, u32[]{:S(2)}) copy-start(s32[4,4]{1,0:T(4,128)} %param.18) | copy-start | bytes 196
  546.0 180.7 %copy-start.38 = (bf16[2,24]{1,0:T(2,128)(2,1)S(1)}, bf16[2,24]{1,0:T(2,128)(2,1)}, u32[]{:S(2)}) copy-start(bf16[2,24]{1,0:T(2,128)(2,1)} %get-tuple-element.79) | copy-start | bytes 292
  546.0 181.2 %copy-start.26 = (bf16[192,96]{1,0:T(8,128)(2,1)S(1)}, bf16[192,96]{1,0:T(8,128)(2,1)}, u32[]{:S(2)}) copy-start(bf16[192,96]{1,0:T(8,128)(2,1)} %get-tuple-element.77) | copy-start | bytes 110596
  (20 other events, 46.8 us)
Sparse Core Ops, SparseCore 0:
  10.8 79.1 all-gather.3
  248.9 60.8 reduce-scatter.12
  313.1 61.6 reduce-scatter.10
  377.9 62.2 reduce-scatter.16
  444.0 61.6 reduce-scatter.14
  508.8 29.7 all-reduce.6
  542.2 181.7 reduce-scatter.18
  726.9 33.2 all-reduce.4
where the time goes:
time: 773 us; the launch traced here: 769 us
  waiting for transfers between devices  430 us (56%)
  blocking collectives  173 us (22%)
  local copies, waits for them, and re-layouts  83.3 us (11%)
  matrix products  42.2 us (5%)
  other arithmetic  19.5 us (3%)
  between operations  15.7 us (2%)
    unnamed x10, waiting for transfers between devices  238 us
    reduce_scatter x1, waiting for transfers between devices, shards(): lax.psum_scatter(param_grads[3], 'lon', scatter_dimension=1, tiled=True)  63.8 us
    reduce_scatter x1, waiting for transfers between devices, shards(): lax.psum_scatter(param_grads[0], 'lon', scatter_dimension=1, tiled=True)  63.6 us
    all_gather x1, blocking collectives, shards(): lax.all_gather(proj_weight, 'lon', axis=1, tiled=True)  33.6 us
    all_gather x1, blocking collectives, shards(): lax.all_gather(up_weight, 'lon', axis=1, tiled=True)  33.3 us
    all_gather x1, blocking collectives, shards(): lax.all_gather(down_weight, 'lon', axis=1, tiled=True)  32.9 us
    psum x1, waiting for transfers between devices, shards(): lax.psum(table_shard.astype(jnp.bfloat16), 'lat').astype(jnp.float32)  32.3 us
    all_gather x1, blocking collectives, shards(): lax.all_gather(qkv_weight, 'lon', axis=1, tiled=True)  31.9 us
  transfers between devices with their start and end apart: 12, of which 9 were waited for; matrix products, arithmetic and copies ran while one was open for 9% of the time, Pallas kernels for 0%

commit v1 on v0

v1 whole, which is shorter than its diff:
```python
import functools
import math

import jax
import jax.numpy as jnp
from jax import lax
from jax.experimental import pallas as pl
from jax.experimental.pallas import tpu as pltpu
from jax.sharding import PartitionSpec as P

WPL = 2
WLAT = 6
WLON = 12
WIN = 144
MESH = pl.DeviceIdType.MESH
F32 = jnp.float32
BF16 = jnp.bfloat16


def layer_norm(values):
    row_mean = jnp.mean(values, axis=-1, keepdims=True)
    centred = values - row_mean
    variance = jnp.mean(centred * centred, axis=-1, keepdims=True)
    inv_std = lax.rsqrt(variance + 1e-05)
    return (centred * inv_std, inv_std)


def norm_back(d_normed, normed, inv_std):
    return inv_std * (
        d_normed
        - jnp.mean(d_normed, axis=-1, keepdims=True)
        - normed * jnp.mean(d_normed * normed, axis=-1, keepdims=True)
    )


def gelu_pair(pre_act):
    cumul = 0.5 * (1.0 + lax.erf(pre_act * 0.7071067811865476))
    density = jnp.exp(-0.5 * pre_act * pre_act) * 0.3989422804014327
    return (pre_act * cumul, cumul + pre_act * density)


def position(nlat, nlon):
    lat, lon = lax.axis_index("lat"), lax.axis_index("lon")

    def at(dlat, dlon):
        return (lax.rem(lat + dlat + nlat, nlat), lax.rem(lon + dlon + nlon, nlon))

    return lat, lon, at


def greet(nlat, nlon, at):
    barrier = pltpu.get_barrier_semaphore()
    peers = [(0, d) for d in range(1, nlon)] + [(d, 0) for d in range(1, nlat)] + [(1, 1), (-1, -1)]
    for peer in peers:
        pl.semaphore_signal(barrier, inc=1, device_id=at(*peer), device_id_type=MESH)
    pl.semaphore_wait(barrier, len(peers))


def send(src, dst, send_sem, recv_sem, device):
    copy = pltpu.make_async_remote_copy(
        src_ref=src, dst_ref=dst, send_sem=send_sem, recv_sem=recv_sem, device_id=device, device_id_type=MESH
    )
    copy.start()
    return copy


def gather_kernel(nlat, nlon, a, d, b, h_lat, h_lon, h_diag, a_all, d_all, b_all, r_lat, r_lon, r_diag,
                  send_sem, recv_sem, hs_sem, hr_sem):
    lat, lon, at = position(nlat, nlon)
    greet(nlat, nlon, at)
    copies = []
    halos = ((h_lat, r_lat, (-1, 0)), (h_lon, r_lon, (0, -1)), (h_diag, r_diag, (-1, -1)))
    for i, (src, dst, step) in enumerate(halos):
        copies.append(send(src, dst, hs_sem.at[i], hr_sem.at[i], at(*step)))
    for step in range(1, nlon):
        for i, (src, dst) in enumerate(((a, a_all), (d, d_all), (b, b_all))):
            copies.append(send(src, dst.at[lon], send_sem.at[i, step], recv_sem.at[i, step], at(0, step)))
    a_all[lon] = a[...]
    d_all[lon] = d[...]
    b_all[lon] = b[...]
    for copy in copies:
        copy.wait()


def reduce_kernel(nlat, nlon, scale, a, d, t, kron, h_lat, h_lon, h_diag, a_out, d_out, t_out, r_lat, r_lon, r_diag,
                  a_in, d_in, t_in, a_row, d_row, t_row, send_sem, recv_sem, ls_sem, lr_sem, hs_sem, hr_sem):
    lat, lon, at = position(nlat, nlon)
    greet(nlat, nlon, at)
    firsts, seconds, halo_copies = [], [], []
    for step in range(1, nlon):
        peer = at(0, step)
        for i, (src, dst) in enumerate(((a, a_in), (d, d_in), (t, t_in))):
            firsts.append(send(src.at[peer[1]], dst.at[step], send_sem.at[i, step], recv_sem.at[i, step], peer))
    halos = ((h_lat, r_lat, (1, 0)), (h_lon, r_lon, (0, 1)), (h_diag, r_diag, (1, 1)))
    for i, (src, dst, step) in enumerate(halos):
        halo_copies.append(send(src, dst, hs_sem.at[i], hr_sem.at[i], at(*step)))
    for copy in firsts:
        copy.wait()
    for i, (own, got, row) in enumerate(((a, a_in, a_row), (d, d_in, d_row), (t, t_in, t_row))):
        total = own[lon].astype(F32)
        for step in range(1, nlon):
            total = total + got[step].astype(F32)
        row[lat] = total.astype(BF16)
    for step in range(1, nlat):
        for i, row in enumerate((a_row, d_row, t_row)):
            seconds.append(send(row.at[lat], row.at[lat], ls_sem.at[i, step], lr_sem.at[i, step], at(step, 0)))
    for copy in halo_copies + seconds:
        copy.wait()
    for row, out in ((a_row, a_out), (d_row, d_out)):
        total = row[0].astype(F32)
        for i in range(1, nlat):
            total = total + row[i].astype(F32)
        out[...] = total * scale
    total = jnp.zeros(t_out.shape, F32)
    for i in range(nlat):
        total = total + jnp.dot(kron[i], t_row[i], preferred_element_type=F32)
    t_out[...] = total


def comm_call(kernel, collective_id, outs, scratch, operands):
    vmem = pl.BlockSpec(memory_space=pltpu.VMEM)
    return pl.pallas_call(
        kernel,
        out_shape=[jax.ShapeDtypeStruct(*o) for o in outs],
        in_specs=[vmem] * len(operands),
        out_specs=[vmem] * len(outs),
        scratch_shapes=scratch,
        compiler_params=pltpu.CompilerParams(
            collective_id=collective_id, has_side_effects=True, vmem_limit_bytes=48 * 2**20
        ),
    )(*operands)


def to_windows(grid):
    p, l, c = grid.shape[:3]
    shaped = grid.reshape(p // WPL, WPL, l // WLAT, WLAT, c // WLON, WLON, grid.shape[-1])
    return shaped.transpose(4, 0, 2, 1, 3, 5, 6).reshape(-1, grid.shape[-1])


def from_windows(flat, p, l, c):
    shaped = flat.reshape(c // WLON, p // WPL, l // WLAT, WPL, WLAT, WLON, flat.shape[-1])
    return shaped.transpose(1, 3, 2, 4, 0, 5, 6).reshape(p, l, c, flat.shape[-1])


def block_grads(cells, cots, qkv_t, proj_t, up_t, down_t, gains, bias, labels):
    features = cells.shape[1]
    positions, head_count = bias.shape[:2]
    head_size = features // head_count
    lon_windows = cells.shape[0] // (positions * WIN)
    factor = 1.0 / math.sqrt(head_size)
    gain_one, gain_two = gains[0].astype(F32), gains[1].astype(F32)

    def by_t(x, w_t):
        return lax.dot_general(x, w_t, (((1,), (1,)), ((), ())), preferred_element_type=F32)

    def outer(x, y):
        return lax.dot_general(x, y, (((0,), (0,)), ((), ())), preferred_element_type=F32)

    window_cells = cells.astype(F32)
    normed_one, inv_one = layer_norm(window_cells)
    scaled_one = (normed_one * gain_one).astype(BF16)
    packed = by_t(scaled_one, qkv_t).astype(BF16)
    packed = packed.reshape(lon_windows, positions, WIN, 3, head_count, head_size)
    queries, key_rows, value_rows = packed[:, :, :, 0], packed[:, :, :, 1], packed[:, :, :, 2]
    scores = jnp.einsum("eathd,eashd->eahts", queries, key_rows, preferred_element_type=F32) * factor
    scores = scores + bias.astype(F32)
    same = labels[:, None, :, None] == labels[:, None, None, :]
    scores = jnp.where(same, scores, -jnp.inf)
    raised = jnp.exp(scores - jnp.max(scores, axis=-1, keepdims=True))
    probs = raised / jnp.sum(raised, axis=-1, keepdims=True)
    probs_b = probs.astype(BF16)
    attended = jnp.einsum("eahts,eashd->eathd", probs_b, value_rows, preferred_element_type=F32)
    attended = attended.astype(BF16).reshape(-1, features)
    middle = window_cells + by_t(attended, proj_t)
    normed_two, inv_two = layer_norm(middle)
    scaled_two = (normed_two * gain_two).astype(BF16)
    pre_act = by_t(scaled_two, up_t)
    activated, slope = gelu_pair(pre_act)
    hidden_b = activated.astype(BF16)
    g_down_t = outer(cots, hidden_b)
    d_hidden = (jnp.dot(cots, down_t, preferred_element_type=F32) * slope).astype(BF16)
    g_up_t = outer(d_hidden, scaled_two)
    d_htwo = jnp.dot(d_hidden, up_t, preferred_element_type=F32)
    g_gain_two = jnp.sum(d_htwo * normed_two, axis=0)
    d_middle = cots.astype(F32) + norm_back(d_htwo * gain_two, normed_two, inv_two)
    d_middle_b = d_middle.astype(BF16)
    g_proj_t = outer(d_middle_b, attended)
    d_att = jnp.dot(d_middle_b, proj_t, preferred_element_type=F32).astype(BF16)
    d_att = d_att.reshape(lon_windows, positions, WIN, head_count, head_size)
    d_prob = jnp.einsum("eathd,eashd->eahts", d_att, value_rows, preferred_element_type=F32)
    d_values = jnp.einsum("eahts,eathd->eashd", probs_b, d_att, preferred_element_type=F32)
    d_score = probs * (d_prob - jnp.sum(probs * d_prob, axis=-1, keepdims=True))
    d_score_b = d_score.astype(BF16)
    d_queries = jnp.einsum("eahts,eashd->eathd", d_score_b, key_rows, preferred_element_type=F32) * factor
    d_keys = jnp.einsum("eahts,eathd->eashd", d_score_b, queries, preferred_element_type=F32) * factor
    d_packed = jnp.stack([d_queries, d_keys, d_values], axis=3).astype(BF16).reshape(-1, 3 * features)
    g_qkv_t = outer(d_packed, scaled_one)
    d_hone = jnp.dot(d_packed, qkv_t, preferred_element_type=F32)
    g_gain_one = jnp.sum(d_hone * normed_one, axis=0)
    d_cells = d_middle + norm_back(d_hone * gain_one, normed_one, inv_one)
    table = jnp.sum(d_score, axis=0)
    gains_grad = jnp.stack([g_gain_one, g_gain_two])
    return d_cells.astype(BF16), g_qkv_t, g_proj_t, g_up_t, g_down_t, gains_grad, table


def shards(inputs, cotangent, qkv_weight, proj_weight, up_weight, down_weight, norm_gains, bias_table, type_of, region):
    levels, rows, cols, features = inputs.shape
    nlat, nlon = lax.axis_size("lat"), lax.axis_size("lon")
    level_windows, row_windows = levels // WPL, rows // WLAT
    type_count, head_count, part = bias_table.shape
    positions = level_windows * row_windows
    lat_index = lax.axis_index("lat")
    row_half, col_half, level_shift = WLAT // 2, WLON // 2, WPL // 2
    all_types = type_of.reshape(level_windows, nlat, row_windows).transpose(1, 0, 2).reshape(nlat, positions)
    types = lax.dynamic_index_in_dim(all_types, lat_index, 0, keepdims=False)
    cuts = [up_weight.shape[1], qkv_weight.shape[1], proj_weight.shape[1], 8]
    starts = [sum(cuts[:i]) for i in range(4)]
    gain_rows = jnp.zeros((8, features), BF16).at[:2, : norm_gains.shape[1]].set(norm_gains)
    a_part = jnp.concatenate([up_weight.T, qkv_weight.T, proj_weight.T, gain_rows], axis=0)
    d_part = down_weight.T
    b_part = jnp.concatenate(
        [lax.dynamic_index_in_dim(bias_table, types[i], 0, keepdims=False) for i in range(positions)], axis=0
    )
    both = jnp.roll(jnp.stack([inputs, cotangent]), -level_shift, axis=1)
    rim_lat = both[:, :, :row_half, col_half:]
    rim_lon = both[:, :, row_half:, :col_half]
    rim_diag = both[:, :, :row_half, :col_half]
    flat = [r.reshape(-1, features) for r in (rim_lat, rim_lon, rim_diag)]
    dma = pltpu.SemaphoreType.DMA
    a_all, d_all, b_all, r_lat, r_lon, r_diag = comm_call(
        functools.partial(gather_kernel, nlat, nlon),
        0,
        [((nlon,) + x.shape, BF16) for x in (a_part, d_part, b_part)] + [(x.shape, BF16) for x in flat],
        [dma((3, nlon)), dma((3, nlon)), dma((3,)), dma((3,))],
        (a_part, d_part, b_part, *flat),
    )
    up_t, qkv_t, proj_t = (
        a_all[:, s : s + c].reshape(nlon * c, features) for s, c in zip(starts[:3], cuts[:3])
    )
    gains = a_all[:, starts[3] : starts[3] + 2, : norm_gains.shape[1]].transpose(1, 0, 2).reshape(2, features)
    down_t = d_all.reshape(nlon * d_all.shape[1], -1)
    bias = b_all.transpose(1, 0, 2).reshape(positions, head_count, WIN, WIN)
    top = jnp.concatenate([both[:, :, row_half:, col_half:], r_lon.reshape(rim_lon.shape)], axis=3)
    bottom = jnp.concatenate([r_lat.reshape(rim_lat.shape), r_diag.reshape(rim_diag.shape)], axis=3)
    shifted = jnp.concatenate([top, bottom], axis=2)
    labels = region.reshape(level_windows, WPL, row_windows, WLAT).transpose(0, 2, 1, 3)
    labels = jnp.broadcast_to(labels[..., None], labels.shape + (WLON,)).reshape(positions, WIN)
    d_cells, g_qkv_t, g_proj_t, g_up_t, g_down_t, g_gains, table = block_grads(
        to_windows(shifted[0]), to_windows(shifted[1]), qkv_t, proj_t, up_t, down_t, gains, bias, labels
    )
    gain_cols = norm_gains.shape[1]
    g_gain_rows = g_gains.reshape(2, nlon, gain_cols).transpose(1, 0, 2)
    g_gain_rows = jnp.zeros((nlon, 8, features), F32).at[:, :2, :gain_cols].set(g_gain_rows)
    ga = jnp.concatenate(
        [g.reshape(nlon, -1, features) for g in (g_up_t, g_qkv_t, g_proj_t)] + [g_gain_rows], axis=1
    ).astype(BF16)
    gd = g_down_t.reshape(nlon, -1, g_down_t.shape[1]).astype(BF16)
    gt = table.astype(BF16).reshape(positions * head_count, nlon, part).transpose(1, 0, 2)
    onehot = (all_types[:, None, :] == jnp.arange(type_count, dtype=jnp.int32)[None, :, None]).astype(BF16)
    kron = jnp.einsum("lyp,gh->lygph", onehot, jnp.eye(head_count, dtype=BF16)).reshape(
        nlat, type_count * head_count, positions * head_count
    )
    back = from_windows(d_cells, levels, rows, cols)
    out_lat = back[:, rows - row_half :, : cols - col_half]
    out_lon = back[:, : rows - row_half, cols - col_half :]
    out_diag = back[:, rows - row_half :, cols - col_half :]
    flat = [r.reshape(-1, features) for r in (out_lat, out_lon, out_diag)]
    token_count = levels * rows * cols * nlat * nlon
    a_sum, d_sum, t_sum, r_lat, r_lon, r_diag = comm_call(
        functools.partial(reduce_kernel, nlat, nlon, 1.0 / math.sqrt(token_count)),
        1,
        [(ga.shape[1:], F32), (gd.shape[1:], F32), ((type_count * head_count, part), F32)]
        + [(x.shape, BF16) for x in flat],
        [pltpu.VMEM(x.shape, BF16) for x in (ga, gd, gt)]
        + [pltpu.VMEM((nlat,) + x.shape[1:], BF16) for x in (ga, gd, gt)]
        + [dma((3, nlon)), dma((3, nlon)), dma((3, nlat)), dma((3, nlat)), dma((3,)), dma((3,))],
        (ga, gd, gt, kron, *flat),
    )
    own = back[:, : rows - row_half, : cols - col_half]
    top = jnp.concatenate([r_diag.reshape(out_diag.shape), r_lat.reshape(out_lat.shape)], axis=2)
    bottom = jnp.concatenate([r_lon.reshape(out_lon.shape), own], axis=2)
    grad_input = jnp.roll(jnp.concatenate([top, bottom], axis=1), level_shift, axis=0)
    g_up, g_qkv, g_proj = (a_sum[s : s + c].T for s, c in zip(starts[:3], cuts[:3]))
    return (
        grad_input,
        g_qkv,
        g_proj,
        g_up,
        d_sum.T,
        a_sum[starts[3] : starts[3] + 2, :gain_cols],
        t_sum.reshape(type_count, head_count, part),
    )


def solution(mesh):
    return jax.shard_map(
        shards,
        mesh=mesh,
        in_specs=(
            P(None, "lat", "lon", None),
            P(None, "lat", "lon", None),
            P(None, "lon"),
            P(None, "lon"),
            P(None, "lon"),
            P(None, "lon"),
            P(None, "lon"),
            P(None, None, "lon"),
            P(),
            P(None, "lat"),
        ),
        out_specs=(
            P(None, "lat", "lon", None),
            P(None, "lon"),
            P(None, "lon"),
            P(None, "lon"),
            P(None, "lon"),
            P(None, "lon"),
            P(None, None, "lon"),
        ),
        check_vma=False,
    )
```

time: 773 us -> 237 us (0.31)
  the two profiles are of different devices: /device:TPU:0 before, /device:TPU:11 now
where the time goes in v1:
time: 237 us; the launch traced here: 235 us
  Pallas kernels  123 us (52%)
  local copies, waits for them, and re-layouts  64.8 us (27%)
  matrix products  27.1 us (11%)
  other arithmetic  13.1 us (6%)
  between operations  7.21 us (3%)
    pallas_call x2, Pallas kernels, comm_call(): pl.pallas_call(kernel, out_shape=[jax.ShapeDtypeStruct(*o) for o in outs]...  123 us
    unnamed x81, local copies, waits for them, and re-layouts  12 us
    convert_element_type x3, local copies, waits for them, and re-layouts, block_grads(): scores = scores + bias.astype(F32)  8.62 us
    convert_element_type x2, local copies, waits for them, and re-layouts, shards(): table.astype(BF16).reshape(positions * head_count, nlon, part)  5.26 us
    convert_element_type x2, local copies, waits for them, and re-layouts, block_grads(): jnp.stack([d_queries, d_keys, d_values], axis=3).astype(BF16)  5.24 us
    dot_general x1, matrix products, block_grads(): jnp.einsum('eahts,eathd->eashd', probs_b, d_att, preferred_element_type=F32)  4.83 us

profile of v1, /device:TPU:11, one launch (start us, length us, event | category | flops | bytes accessed | tf_op | source)
XLA Modules:
  0.0 235.5 jit_solution(5682153176858482146)
XLA Ops:
  12.3 1.6 constant_dynamic-slice_fusion.3
  16.2 57.7 %shard_map.153 = (bf16[8,200,192]{2,1,0:T(8,128)(2,1)S(1)}, bf16[8,24,768]{2,1,0:T(8,128)(2,1)S(1)}, bf16[8,24,2592]{2,1,0:T(8,128)(2,1)S(1)}, bf16[288,192]{1,0...) custom-call(bf16[200,192]{1,0:T(8,128)(2,1)S(1)} %fusion.26.a, ...), custom_call_target="tpu_custom_call" | custom-call | tf_op jit(solution)/shard_map/pallas_call | solution.py:122
  75.7 1.4 maximum_maximum_fusion
  82.7 1.1 reshape_transpose_reshape_squeeze.4
  85.6 1.0 copy.61
  86.6 1.4 convolution_convert_fusion
  89.2 1.3 fusion.34
  91.0 2.6 %reshape.487 = f32[4,6,144,144]{3,2,1,0:T(8,128)} reshape(f32[24,8,2592]{2,1,0:T(8,128)S(1)} %copy.57) | data formatting | bytes 3981312 | tf_op jit(solution)/shard_map/convert_element_type | solution.py:166
  93.6 5.6 %copy.58 = f32[4,6,144,144]{2,3,1,0:T(8,128)} copy(f32[4,6,144,144]{3,2,1,0:T(8,128)} %reshape.487) | data formatting | bytes 3981312 | tf_op jit(solution)/shard_map/convert_element_type | solution.py:166
  99.2 2.8 %add_select_fusion = f32[4,6,144,144]{2,3,1,0:T(8,128)S(1)} fusion(f32[4,6,144,144]{2,3,1,0:T(8,128)} %copy.58, pred[4,144,144]{1,2,0:T(8,128)(4,1)S(1)} %copy-done.24, bf16[1,4,144,1,6,32]{2,1,5,4,3,0:T(4,128)(2,1)S(1)} %get-tuple-element.80, bf16[1,4,144,1,6,32]{2,1,5,4,3,0:T(4,128)(2,1)S(1)} %get-tuple-element.79), kind=kOutput, calls=%fused_computation.4 | convolution fusion | flops 33343488 | bytes 4506624 | tf_op jit(solution)/shard_map/eathd,eashd->eahts/dot_general | solution.py:165
  102.0 1.8 copy-done.8
  103.8 2.4 %fusion.39 = (f32[4,6,144]{2,1,0:T(8,128)S(1)}, f32[4,6,144,144]{2,3,1,0:T(8,128)}) fusion(f32[4,6,144,144]{2,3,1,0:T(8,128)S(1)} %add_select_fusion), kind=kOutput, calls=%fused_computation.120 | output fusion | flops 995471 | bytes 3995136 | tf_op jit(solution)/shard_map/sub | solution.py:169
  106.2 4.1 %fusion.10 = bf16[1,4,144,6,32]{2,4,3,1,0:T(8,128)(2,1)S(1)} fusion(bf16[1,4,144,1,6,32]{2,1,5,4,3,0:T(4,128)(2,1)S(1)} %copy-done.25, f32[4,6,144]{2,1,0:T(8,128)S(1)} %get-tuple-element.99, f32[4,6,144,144]{2,3,1,0:T(8,128)} %copy-done.8), kind=kOutput, calls=%fused_computation.30 | convolution fusion | flops 33457680 | bytes 2446848 | tf_op jit(solution)/shard_map/eahts,eashd->eathd/dot_general | solution.py:172
  110.7 1.0 reshape.490
  119.4 4.8 %convolution_bitcast_fusion = bf16[1,4,144,1,6,32]{2,5,4,1,3,0:T(8,128)(2,1)} fusion(bf16[4,144,6,32]{1,0,3,2:T(4,128)(2,1)S(1)} %reshape.475, f32[4,6,144]{2,1,0:T(8,128)S(1)} %get-tuple-element.99, f32[4,6,144,144]{2,3,1,0:T(8,128)} %copy-done.8), kind=kOutput, calls=%fused_computation.20 | convolution fusion | flops 33347088 | bytes 2446848 | tf_op jit(solution)/shard_map/eahts,eathd->eashd/dot_general | solution.py:191
  124.3 2.9 %multiply_reduce_fusion = (f32[4,6,144]{2,1,0:T(8,128)S(1)}, f32[4,6,144,144]{2,3,1,0:T(8,128)S(1)}) fusion(f32[4,6,144,144]{2,3,1,0:T(8,128)} %get-tuple-element.100, f32[4,6,144]{2,1,0:T(8,128)S(1)} %get-tuple-element.99, bf16[1,4,144,1,6,32]{2,1,5,4,3,0:T(4,128)(2,1)S(1)} %copy-done.26, bf16[4,144,6,32]{1,0,3,2:T(4,128)(2,1)S(1)} %reshape.475), kind=kOutput, calls=%fused_computation.2 | convolution fusion | flops 33340032 | bytes 4451328 | tf_op jit(solution)/shard_map/eathd,eashd->eahts/dot_general | solution.py:190
  129.3 1.1 fusion.9
  130.5 2.4 %copy.75 = bf16[4,6,144,144]{3,2,1,0:T(8,128)(2,1)} copy(bf16[4,6,144,144]{2,3,1,0:T(8,128)(2,1)S(1)} %multiply_convert_fusion) | data formatting | bytes 1990656 | tf_op jit(solution)/shard_map/convert_element_type | solution.py:193
  132.9 3.9 %convert_element_type.149 = bf16[24,8,2592]{2,1,0:T(8,128)(2,1)} reshape(bf16[4,6,144,144]{3,2,1,0:T(8,128)(2,1)} %copy.75) | data formatting | bytes 1990656 | tf_op jit(solution)/shard_map/convert_element_type | solution.py:258
  136.8 1.4 copy.120
  138.5 2.0 copy.69
  140.5 3.2 %convert_element_type.146 = bf16[576,576]{0,1:T(8,128)(2,1)} reshape(bf16[1,4,144,3,6,32]{2,1,5,4,3,0:T(4,128)(2,1)} %copy.69) | data formatting | bytes 1327104 | tf_op jit(solution)/shard_map/convert_element_type | solution.py:196
  143.8 2.3 convolution_convert_fusion.4
  146.0 2.5 %multiply_reduce_fusion.4 = (bf16[192]{0:T(256)(128)(2,1)S(1)}, f32[576]{0:T(1024)S(1)}, f32[576]{0:T(1024)S(1)}, f32[576,192]{0,1:T(8,128)}) fusion(f32[576,192]{0,1:T(8,128)S(1)} %copy-done.10, f32[576]{0:T(1024)S(1)} %copy-done.34, f32[576]{0:T(1024)S(1)} %copy-done.33, f32[192]{0:T(256)S(1)} %copy-done.37, bf16[576,576]{0,1:T(8,128)(2,1)} %convert_element_type.146, ...), kind=kOutput, calls=%fused_computation.50 | convolution fusion | flops 128285376 | bytes 1779840 | tf_op jit(solution)/shard_map/dot_general | solution.py:198
  148.7 1.4 add_convert_fusion
  150.0 1.3 fusion.15.a
  152.5 65.6 %shard_map.154 = (f32[200,192]{1,0:T(8,128)S(1)}, f32[24,768]{1,0:T(8,128)S(1)}, f32[96,2592]{1,0:T(8,128)S(1)}, bf16[144,192]{1,0:T(8,128)(2,1)S(1)}, bf16[144,...) custom-call(bf16[8,200,192]{2,1,0:T(8,128)(2,1)S(1)} %fusion.15.a, ...), custom_call_target="tpu_custom_call" | custom-call | tf_op jit(solution)/shard_map/pallas_call | solution.py:122
  222.8 1.4 slice_bitcast_fusion.2
  224.1 1.5 slice_bitcast_fusion.1
  229.1 1.1 fusion.19
  231.1 1.2 reshape.484
  232.3 2.5 %copy.82 = f32[16,6,2592]{2,0,1:T(8,128)} copy(f32[16,6,2592]{2,1,0:T(8,128)} %reshape.484) | data formatting | bytes 1990656
  (164 shorter events, 39.9 us)
Async XLA Ops:
  0.6 14.0 %copy-start.28 = (bf16[8,6,12,192]{3,0,2,1:T(8,128)(2,1)S(1)}, bf16[8,6,12,192]{3,0,2,1:T(8,128)(2,1)}, u32[]{:S(2)}) copy-start(bf16[8,6,12,192]{3,0,2,1:T(8,128)(2,1)} %param.15) | copy-start | bytes 663556
  0.6 14.0 %copy-start.29 = (bf16[8,6,12,192]{3,0,2,1:T(8,128)(2,1)S(1)}, bf16[8,6,12,192]{3,0,2,1:T(8,128)(2,1)}, u32[]{:S(2)}) copy-start(bf16[8,6,12,192]{3,0,2,1:T(8,128)(2,1)} %param.14) | copy-start | bytes 663556
  15.1 1.1 copy-start.6
  74.2 6.5 %copy-start.36 = (f32[192]{0:T(256)}, f32[192]{0:T(256)S(1)}, u32[]{:S(2)}) copy-start(f32[192]{0:T(256)S(1)} %reshape.486) | copy-start | bytes 2308
  83.8 2.8 %copy-start.16 = (bf16[576,192]{1,0:T(8,128)(2,1)}, bf16[576,192]{1,0:T(8,128)(2,1)S(1)}, u32[]{:S(2)}) copy-start(bf16[576,192]{1,0:T(8,128)(2,1)S(1)} %reshape_transpose_reshape_squeeze.4) | copy-start | bytes 663556
  83.8 2.8 %copy-start.18 = (bf16[576,192]{1,0:T(8,128)(2,1)S(1)}, bf16[576,192]{1,0:T(8,128)(2,1)}, u32[]{:S(2)}) copy-start(bf16[576,192]{1,0:T(8,128)(2,1)} %convert_element_type.128) | copy-start | bytes 663556
  90.4 8.8 %copy-start.11 = (bf16[1,4,144,1,6,32]{2,1,5,4,3,0:T(4,128)(2,1)}, bf16[1,4,144,1,6,32]{2,1,5,4,3,0:T(4,128)(2,1)S(1)}, u32[]{:S(2)}) copy-start(bf16[1,4,144,1,6,32]{2,1,5,4,3,0:T(4,128)(2,1)S(1)} %get-tuple-element.79) | copy-start | bytes 663556
  90.4 8.8 %copy-start.13 = (bf16[1,4,144,1,6,32]{2,1,5,4,3,0:T(4,128)(2,1)}, bf16[1,4,144,1,6,32]{2,1,5,4,3,0:T(4,128)(2,1)S(1)}, u32[]{:S(2)}) copy-start(bf16[1,4,144,1,6,32]{2,1,5,4,3,0:T(4,128)(2,1)S(1)} %get-tuple-element.80) | copy-start | bytes 663556
  93.6 5.6 %copy-start.24 = (pred[4,144,144]{1,2,0:T(8,128)(4,1)S(1)}, pred[4,144,144]{1,2,0:T(8,128)(4,1)}, u32[]{:S(2)}) copy-start(pred[4,144,144]{1,2,0:T(8,128)(4,1)} %broadcast_compare_fusion) | copy-start | bytes 248836
  102.0 1.8 copy-start.8
  103.8 2.4 %copy-start.25 = (bf16[1,4,144,1,6,32]{2,1,5,4,3,0:T(4,128)(2,1)S(1)}, bf16[1,4,144,1,6,32]{2,1,5,4,3,0:T(4,128)(2,1)}, u32[]{:S(2)}) copy-start(bf16[1,4,144,1,6,32]{2,1,5,4,3,0:T(4,128)(2,1)} %get-tuple-element.81) | copy-start | bytes 663556
  110.4 1.6 copy-start.9
  110.4 1.9 copy-start.15
  113.1 1.0 copy-start.17
  114.9 2.8 %copy-start.20 = (bf16[576,192]{0,1:T(8,128)(2,1)S(1)}, bf16[576,192]{0,1:T(8,128)(2,1)}, u32[]{:S(2)}) copy-start(bf16[576,192]{0,1:T(8,128)(2,1)} %copy.63) | copy-start | bytes 663556
  115.6 2.3 copy-start.23
  116.8 2.7 %copy-start.31 = (f32[576]{0:T(1024)}, f32[576]{0:T(1024)S(1)}, u32[]{:S(2)}) copy-start(f32[576]{0:T(1024)S(1)} %broadcast_multiply_fusion.4) | copy-start | bytes 6916
  119.4 4.8 %copy-start.26 = (bf16[1,4,144,1,6,32]{2,1,5,4,3,0:T(4,128)(2,1)S(1)}, bf16[1,4,144,1,6,32]{2,1,5,4,3,0:T(4,128)(2,1)}, u32[]{:S(2)}) copy-start(bf16[1,4,144,1,6,32]{2,1,5,4,3,0:T(4,128)(2,1)} %get-tuple-element.81) | copy-start | bytes 663556
  124.3 3.1 %copy-start.7 = (f32[4,6,144,144]{2,3,1,0:T(8,128)S(1)}, f32[4,6,144,144]{2,3,1,0:T(8,128)}, u32[]{:S(2)}) copy-start(f32[4,6,144,144]{2,3,1,0:T(8,128)} %get-tuple-element.100) | copy-start | bytes 5971972
  127.3 1.0 copy-start.14
  128.3 1.0 copy-start.12
  132.9 5.3 %copy-start.22 = (bf16[1,4,144,1,6,32]{2,5,4,1,3,0:T(8,128)(2,1)S(1)}, bf16[1,4,144,1,6,32]{2,5,4,1,3,0:T(8,128)(2,1)}, u32[]{:S(2)}) copy-start(bf16[1,4,144,1,6,32]{2,5,4,1,3,0:T(8,128)(2,1)} %fusion.9) | copy-start | bytes 663556
  136.8 1.4 copy-start.27
  138.5 5.3 %copy-start.19 = (bf16[576,192]{1,0:T(8,128)(2,1)S(1)}, bf16[576,192]{1,0:T(8,128)(2,1)}, u32[]{:S(2)}) copy-start(bf16[576,192]{1,0:T(8,128)(2,1)} %convert_element_type.128) | copy-start | bytes 663556
  140.5 5.5 %copy-start.10 = (f32[576,192]{0,1:T(8,128)S(1)}, f32[576,192]{0,1:T(8,128)}, u32[]{:S(2)}) copy-start(f32[576,192]{0,1:T(8,128)} %copy.61) | copy-start | bytes 1327108
  140.5 5.5 %copy-start.33 = (f32[576]{0:T(1024)S(1)}, f32[576]{0:T(1024)}, u32[]{:S(2)}) copy-start(f32[576]{0:T(1024)} %div.43) | copy-start | bytes 6916
  140.5 5.5 %copy-start.34 = (f32[576]{0:T(1024)S(1)}, f32[576]{0:T(1024)}, u32[]{:S(2)}) copy-start(f32[576]{0:T(1024)} %rsqrt.22) | copy-start | bytes 6916
  140.5 5.5 %copy-start.37 = (f32[192]{0:T(256)S(1)}, f32[192]{0:T(256)}, u32[]{:S(2)}) copy-start(f32[192]{0:T(256)} %copy-done.36) | copy-start | bytes 2308
  143.7 4.8 %copy-start.35 = (bf16[1,8,24]{2,0,1:T(2,128)(2,1)S(1)}, bf16[1,8,24]{2,0,1:T(2,128)(2,1)}, u32[]{:S(2)}) copy-start(bf16[1,8,24]{2,0,1:T(2,128)(2,1)} %stack.41) | copy-start | bytes 1156
  143.7 4.9 %copy-start.21 = (bf16[576,192]{0,1:T(8,128)(2,1)S(1)}, bf16[576,192]{0,1:T(8,128)(2,1)}, u32[]{:S(2)}) copy-start(bf16[576,192]{0,1:T(8,128)(2,1)} %copy.63) | copy-start | bytes 663556
  143.7 4.9 %copy-start.32 = (f32[576]{0:T(1024)S(1)}, f32[576]{0:T(1024)}, u32[]{:S(2)}) copy-start(f32[576]{0:T(1024)} %copy-done.31) | copy-start | bytes 6916
  232.3 2.5 %copy-start.2 = (f32[24,768]{1,0:T(8,128)S(1)}, f32[24,768]{1,0:T(8,128)}, u32[]{:S(2)}) copy-start(f32[24,768]{1,0:T(8,128)} %copy-done.1) | copy-start | bytes 221188
  (6 other events, 4.1 us)

commit v2 on v1

--- a/solution.py
+++ b/solution.py
@@ -45,15 +45,23 @@
     def at(dlat, dlon):
         return (lax.rem(lat + dlat + nlat, nlat), lax.rem(lon + dlon + nlon, nlon))
 
-    return lat, lon, at
-
-
-def greet(nlat, nlon, at):
+    core, side = lax.rem(lat, 2), lax.rem(lon, 2)
+    twin = (lat + 1 - 2 * core, lon)
+    across = (lat, lon + 1 - 2 * side)
+    return lat, lon, at, core, twin, across
+
+
+def greet(devices):
     barrier = pltpu.get_barrier_semaphore()
-    peers = [(0, d) for d in range(1, nlon)] + [(d, 0) for d in range(1, nlat)] + [(1, 1), (-1, -1)]
-    for peer in peers:
-        pl.semaphore_signal(barrier, inc=1, device_id=at(*peer), device_id_type=MESH)
-    pl.semaphore_wait(barrier, len(peers))
+    for device in devices:
+        pl.semaphore_signal(barrier, inc=1, device_id=device, device_id_type=MESH)
+    pl.semaphore_wait(barrier, len(devices))
+
+
+def peers(nlat, nlon, at, twin, across):
+    steps = [(0, d) for d in range(2, nlon, 2)] + [(d, 0) for d in range(2, nlat, 2)]
+    steps += [(1, 0), (-1, 0), (0, 1), (0, -1), (1, 1), (-1, -1)]
+    return [twin, across] + [at(*step) for step in steps]
 
 
 def send(src, dst, send_sem, recv_sem, device):
@@ -65,52 +73,119 @@
 
 
 def gather_kernel(nlat, nlon, a, d, b, h_lat, h_lon, h_diag, a_all, d_all, b_all, r_lat, r_lon, r_diag,
-                  send_sem, recv_sem, hs_sem, hr_sem):
-    lat, lon, at = position(nlat, nlon)
-    greet(nlat, nlon, at)
-    copies = []
-    halos = ((h_lat, r_lat, (-1, 0)), (h_lon, r_lon, (0, -1)), (h_diag, r_diag, (-1, -1)))
-    for i, (src, dst, step) in enumerate(halos):
-        copies.append(send(src, dst, hs_sem.at[i], hr_sem.at[i], at(*step)))
-    for step in range(1, nlon):
-        for i, (src, dst) in enumerate(((a, a_all), (d, d_all), (b, b_all))):
-            copies.append(send(src, dst.at[lon], send_sem.at[i, step], recv_sem.at[i, step], at(0, step)))
+                  zs, zr, xs, xr, ts, tr, hs, hr):
+    lat, lon, at, core, twin, across = position(nlat, nlon)
+    greet(peers(nlat, nlon, at, twin, across))
+    reach = nlon // 2
+    srcs = (a.at[core], d.at[core], b)
+
+    def slots(owner):
+        return (a_all.at[owner, core], d_all.at[owner, core], b_all.at[owner])
+
+    far, near, shared, halo = {}, {}, [], []
+    for k in range(1, reach):
+        for i in range(3):
+            far[i, k] = send(srcs[i], slots(lon)[i], zs.at[i, k], zr.at[i, k], at(0, 2 * k))
+    for i in range(3):
+        near[i, 0] = send(srcs[i], slots(lon)[i], xs.at[i, 0], xr.at[i, 0], across)
+    for i, (src, dst, step) in enumerate(
+        ((h_lat, r_lat, (-1, 0)), (h_lon, r_lon, (0, -1)), (h_diag, r_diag, (-1, -1)))
+    ):
+        halo.append(send(src, dst, hs.at[i], hr.at[i], at(*step)))
     a_all[lon] = a[...]
     d_all[lon] = d[...]
     b_all[lon] = b[...]
-    for copy in copies:
+    for k in range(1, reach):
+        owner = lax.rem(lon - 2 * k + nlon, nlon)
+        for i in range(3):
+            slot = slots(owner)[i]
+            far[i, k].wait_recv()
+            near[i, k] = send(slot, slot, xs.at[i, k], xr.at[i, k], across)
+            if i < 2:
+                shared.append(send(slot, slot, ts.at[i, k], tr.at[i, k], twin))
+    for k in range(reach):
+        owner = lax.rem(across[1] - 2 * k + nlon, nlon)
+        for i in range(3):
+            slot = slots(owner)[i]
+            near[i, k].wait_recv()
+            if i < 2:
+                shared.append(send(slot, slot, ts.at[i, reach + k], tr.at[i, reach + k], twin))
+    for copy in list(far.values()) + list(near.values()):
+        copy.wait_send()
+    for copy in halo + shared:
         copy.wait()
 
 
 def reduce_kernel(nlat, nlon, scale, a, d, t, kron, h_lat, h_lon, h_diag, a_out, d_out, t_out, r_lat, r_lon, r_diag,
-                  a_in, d_in, t_in, a_row, d_row, t_row, send_sem, recv_sem, ls_sem, lr_sem, hs_sem, hr_sem):
-    lat, lon, at = position(nlat, nlon)
-    greet(nlat, nlon, at)
-    firsts, seconds, halo_copies = [], [], []
-    for step in range(1, nlon):
-        peer = at(0, step)
-        for i, (src, dst) in enumerate(((a, a_in), (d, d_in), (t, t_in))):
-            firsts.append(send(src.at[peer[1]], dst.at[step], send_sem.at[i, step], recv_sem.at[i, step], peer))
-    halos = ((h_lat, r_lat, (1, 0)), (h_lon, r_lon, (0, 1)), (h_diag, r_diag, (1, 1)))
-    for i, (src, dst, step) in enumerate(halos):
-        halo_copies.append(send(src, dst, hs_sem.at[i], hr_sem.at[i], at(*step)))
-    for copy in firsts:
+                  a_twin, d_twin, a_half, d_half, a_x, d_x, t_x, a_mid, d_mid, t_mid, a_z, d_z, t_z,
+                  a_row, d_row, t_row, cs, cr, xs, xr, zs, zr, ls, lr, fs, fr, hs, hr):
+    lat, lon, at, core, twin, across = position(nlat, nlon)
+    greet(peers(nlat, nlon, at, twin, across))
+    reach = nlon // 2
+    near, far, rest = {}, {}, []
+    order = list(range(1, reach)) + [0]
+    pairs = [
+        send(src.at[1 - core], dst, cs.at[i], cr.at[i], twin)
+        for i, (src, dst) in enumerate(((a, a_twin), (d, d_twin)))
+    ]
+
+    def cross(i, src, dst):
+        for k in order:
+            owner = lax.rem(across[1] + 2 * k, nlon)
+            near[i, k] = send(src.at[owner], dst.at[k], xs.at[i, k], xr.at[i, k], across)
+
+    cross(2, t, t_x)
+    for i, (src, dst, step) in enumerate(
+        ((h_lat, r_lat, (1, 0)), (h_lon, r_lon, (0, 1)), (h_diag, r_diag, (1, 1)))
+    ):
+        rest.append(send(src, dst, hs.at[i], hr.at[i], at(*step)))
+    for i, (own, got, half, dst) in enumerate(((a, a_twin, a_half, a_x), (d, d_twin, d_half, d_x))):
+        pairs[i].wait()
+        half[...] = (own[core].astype(F32) + got[...].astype(F32)).astype(BF16)
+        cross(i, half, dst)
+    streams = ((2, t, t_x, t_mid, t_z), (0, a_half, a_x, a_mid, a_z), (1, d_half, d_x, d_mid, d_z))
+    for i, own, got, mid, dst in streams:
+        for k in range(1, reach):
+            owner = lax.rem(lon + 2 * k, nlon)
+            near[i, k].wait_recv()
+            mid[k] = (own[owner].astype(F32) + got[k].astype(F32)).astype(BF16)
+            far[i, k] = send(mid.at[k], dst.at[k], zs.at[i, k], zr.at[i, k], at(0, 2 * k))
+    rows = nlat // 2
+    row = lax.div(lat, 2)
+
+    def total_of(i, own, got, dst):
+        near[i, 0].wait_recv()
+        total = own[lon].astype(F32) + got[0].astype(F32)
+        for k in range(1, reach):
+            far[i, k].wait_recv()
+            total = total + dst[k].astype(F32)
+        return total.astype(BF16)
+
+    t_row[lat] = total_of(2, t, t_x, t_z)
+    rest.append(send(t_row.at[lat], t_row.at[lat], ls.at[2, 0], lr.at[2, 0], twin))
+    t_far = [send(t_row.at[lat], t_row.at[lat], ls.at[2, j], lr.at[2, j], at(2 * j, 0)) for j in range(1, rows)]
+    halves = []
+    for i, own, got, dst, line in ((0, a_half, a_x, a_z, a_row), (1, d_half, d_x, d_z, d_row)):
+        line[row] = total_of(i, own, got, dst)
+        halves.append(
+            [send(line.at[row], line.at[row], ls.at[i, j], lr.at[i, j], at(2 * j, 0)) for j in range(1, rows)]
+        )
+    for j in range(1, rows):
+        slot = t_row.at[lax.rem(lat - 2 * j + nlat, nlat)]
+        t_far[j - 1].wait_recv()
+        rest.append(send(slot, slot, fs.at[2, j], fr.at[2, j], twin))
+    for i, (line, out) in enumerate(((a_row, a_out), (d_row, d_out))):
+        for copy in halves[i]:
+            copy.wait_recv()
+        total = line[0].astype(F32)
+        for j in range(1, rows):
+            total = total + line[j].astype(F32)
+        out[core] = total * scale
+        rest.append(send(out.at[core], out.at[core], fs.at[i, 0], fr.at[i, 0], twin))
+    for copy in list(near.values()) + list(far.values()) + t_far + halves[0] + halves[1]:
+        copy.wait_send()
+    for copy in rest:
         copy.wait()
-    for i, (own, got, row) in enumerate(((a, a_in, a_row), (d, d_in, d_row), (t, t_in, t_row))):
-        total = own[lon].astype(F32)
-        for step in range(1, nlon):
-            total = total + got[step].astype(F32)
-        row[lat] = total.astype(BF16)
-    for step in range(1, nlat):
-        for i, row in enumerate((a_row, d_row, t_row)):
-            seconds.append(send(row.at[lat], row.at[lat], ls_sem.at[i, step], lr_sem.at[i, step], at(step, 0)))
-    for copy in halo_copies + seconds:
-        copy.wait()
-    for row, out in ((a_row, a_out), (d_row, d_out)):
-        total = row[0].astype(F32)
-        for i in range(1, nlat):
-            total = total + row[i].astype(F32)
-        out[...] = total * scale
     total = jnp.zeros(t_out.shape, F32)
     for i in range(nlat):
         total = total + jnp.dot(kron[i], t_row[i], preferred_element_type=F32)
@@ -213,11 +288,18 @@
     row_half, col_half, level_shift = WLAT // 2, WLON // 2, WPL // 2
     all_types = type_of.reshape(level_windows, nlat, row_windows).transpose(1, 0, 2).reshape(nlat, positions)
     types = lax.dynamic_index_in_dim(all_types, lat_index, 0, keepdims=False)
-    cuts = [up_weight.shape[1], qkv_weight.shape[1], proj_weight.shape[1], 8]
-    starts = [sum(cuts[:i]) for i in range(4)]
-    gain_rows = jnp.zeros((8, features), BF16).at[:2, : norm_gains.shape[1]].set(norm_gains)
-    a_part = jnp.concatenate([up_weight.T, qkv_weight.T, proj_weight.T, gain_rows], axis=0)
-    d_part = down_weight.T
+    n_up, n_qkv, n_proj = up_weight.shape[1], qkv_weight.shape[1], proj_weight.shape[1]
+    gain_cols, height = norm_gains.shape[1], -(-max(n_up + 2, n_qkv + n_proj) // 8) * 8
+    gain_rows = jnp.pad(norm_gains, ((0, height - n_up - 2), (0, features - gain_cols)))
+    a_part = jnp.stack(
+        [
+            jnp.concatenate([up_weight.T, gain_rows]),
+            jnp.pad(
+                jnp.concatenate([qkv_weight.T, proj_weight.T]), ((0, height - n_qkv - n_proj), (0, 0))
+            ),
+        ]
+    )
+    d_part = down_weight.reshape(2, -1, down_weight.shape[1]).transpose(0, 2, 1)
     b_part = jnp.concatenate(
         [lax.dynamic_index_in_dim(bias_table, types[i], 0, keepdims=False) for i in range(positions)], axis=0
     )
@@ -231,14 +313,14 @@
         functools.partial(gather_kernel, nlat, nlon),
         0,
         [((nlon,) + x.shape, BF16) for x in (a_part, d_part, b_part)] + [(x.shape, BF16) for x in flat],
-        [dma((3, nlon)), dma((3, nlon)), dma((3,)), dma((3,))],
+        [dma((3, nlon // 2))] * 4 + [dma((2, nlon))] * 2 + [dma((3,))] * 2,
         (a_part, d_part, b_part, *flat),
     )
-    up_t, qkv_t, proj_t = (
-        a_all[:, s : s + c].reshape(nlon * c, features) for s, c in zip(starts[:3], cuts[:3])
-    )
-    gains = a_all[:, starts[3] : starts[3] + 2, : norm_gains.shape[1]].transpose(1, 0, 2).reshape(2, features)
-    down_t = d_all.reshape(nlon * d_all.shape[1], -1)
+    up_t = a_all[:, 0, :n_up].reshape(-1, features)
+    qkv_t = a_all[:, 1, :n_qkv].reshape(-1, features)
+    proj_t = a_all[:, 1, n_qkv : n_qkv + n_proj].reshape(-1, features)
+    gains = a_all[:, 0, n_up : n_up + 2, :gain_cols].transpose(1, 0, 2).reshape(2, features)
+    down_t = d_all.transpose(0, 2, 1, 3).reshape(features, -1)
     bias = b_all.transpose(1, 0, 2).reshape(positions, head_count, WIN, WIN)
     top = jnp.concatenate([both[:, :, row_half:, col_half:], r_lon.reshape(rim_lon.shape)], axis=3)
     bottom = jnp.concatenate([r_lat.reshape(rim_lat.shape), r_diag.reshape(rim_diag.shape)], axis=3)
@@ -248,13 +330,18 @@
     d_cells, g_qkv_t, g_proj_t, g_up_t, g_down_t, g_gains, table = block_grads(
         to_windows(shifted[0]), to_windows(shifted[1]), qkv_t, proj_t, up_t, down_t, gains, bias, labels
     )
-    gain_cols = norm_gains.shape[1]
     g_gain_rows = g_gains.reshape(2, nlon, gain_cols).transpose(1, 0, 2)
-    g_gain_rows = jnp.zeros((nlon, 8, features), F32).at[:, :2, :gain_cols].set(g_gain_rows)
-    ga = jnp.concatenate(
-        [g.reshape(nlon, -1, features) for g in (g_up_t, g_qkv_t, g_proj_t)] + [g_gain_rows], axis=1
+    g_gain_rows = jnp.pad(g_gain_rows, ((0, 0), (0, height - n_up - 2), (0, features - gain_cols)))
+    g_up_t, g_qkv_t, g_proj_t = (g.reshape(nlon, -1, features) for g in (g_up_t, g_qkv_t, g_proj_t))
+    ga = jnp.stack(
+        [
+            jnp.concatenate([g_up_t, g_gain_rows], axis=1),
+            jnp.pad(
+                jnp.concatenate([g_qkv_t, g_proj_t], axis=1), ((0, 0), (0, height - n_qkv - n_proj), (0, 0))
+            ),
+        ]
     ).astype(BF16)
-    gd = g_down_t.reshape(nlon, -1, g_down_t.shape[1]).astype(BF16)
+    gd = g_down_t.reshape(nlon, -1, 2, g_down_t.shape[1] // 2).transpose(2, 0, 1, 3).astype(BF16)
     gt = table.astype(BF16).reshape(positions * head_count, nlon, part).transpose(1, 0, 2)
     onehot = (all_types[:, None, :] == jnp.arange(type_count, dtype=jnp.int32)[None, :, None]).astype(BF16)
     kron = jnp.einsum("lyp,gh->lygph", onehot, jnp.eye(head_count, dtype=BF16)).reshape(
@@ -265,29 +352,31 @@
     out_lon = back[:, : rows - row_half, cols - col_half :]
     out_diag = back[:, rows - row_half :, cols - col_half :]
     flat = [r.reshape(-1, features) for r in (out_lat, out_lon, out_diag)]
+    shard_shapes = (ga.shape[2:], gd.shape[2:], gt.shape[1:])
     token_count = levels * rows * cols * nlat * nlon
     a_sum, d_sum, t_sum, r_lat, r_lon, r_diag = comm_call(
         functools.partial(reduce_kernel, nlat, nlon, 1.0 / math.sqrt(token_count)),
         1,
-        [(ga.shape[1:], F32), (gd.shape[1:], F32), ((type_count * head_count, part), F32)]
+        [((2,) + ga.shape[2:], F32), ((2,) + gd.shape[2:], F32), ((type_count * head_count, part), F32)]
         + [(x.shape, BF16) for x in flat],
-        [pltpu.VMEM(x.shape, BF16) for x in (ga, gd, gt)]
-        + [pltpu.VMEM((nlat,) + x.shape[1:], BF16) for x in (ga, gd, gt)]
-        + [dma((3, nlon)), dma((3, nlon)), dma((3, nlat)), dma((3, nlat)), dma((3,)), dma((3,))],
+        [pltpu.VMEM(x.shape[1:], BF16) for x in (ga, gd)] * 2
+        + [pltpu.VMEM((nlon // 2,) + shape, BF16) for shape in shard_shapes] * 3
+        + [pltpu.VMEM((nlat // 2,) + shape, BF16) for shape in shard_shapes[:2]]
+        + [pltpu.VMEM((nlat,) + shard_shapes[2], BF16)]
+        + [dma((2,))] * 2 + [dma((3, nlon // 2))] * 4 + [dma((3, nlat // 2))] * 4 + [dma((3,))] * 2,
         (ga, gd, gt, kron, *flat),
     )
     own = back[:, : rows - row_half, : cols - col_half]
     top = jnp.concatenate([r_diag.reshape(out_diag.shape), r_lat.reshape(out_lat.shape)], axis=2)
     bottom = jnp.concatenate([r_lon.reshape(out_lon.shape), own], axis=2)
     grad_input = jnp.roll(jnp.concatenate([top, bottom], axis=1), level_shift, axis=0)
-    g_up, g_qkv, g_proj = (a_sum[s : s + c].T for s, c in zip(starts[:3], cuts[:3]))
     return (
         grad_input,
-        g_qkv,
-        g_proj,
-        g_up,
-        d_sum.T,
-        a_sum[starts[3] : starts[3] + 2, :gain_cols],
+        a_sum[1, :n_qkv].T,
+        a_sum[1, n_qkv : n_qkv + n_proj].T,
+        a_sum[0, :n_up].T,
+        d_sum.transpose(0, 2, 1).reshape(down_weight.shape),
+        a_sum[0, n_up : n_up + 2, :gain_cols],
         t_sum.reshape(type_count, head_count, part),
     )
 

time: 237 us -> 186 us (0.78)
  the two profiles are of different devices: /device:TPU:11 before, /device:TPU:0 now
where the time goes in v2:
time: 186 us; the launch traced here: 184 us
  Pallas kernels  73.5 us (40%)
  local copies, waits for them, and re-layouts  65.2 us (35%)
  matrix products  26 us (14%)
  other arithmetic  12.4 us (7%)
  between operations  7.39 us (4%)
    pallas_call x2, Pallas kernels, comm_call(): pl.pallas_call(kernel, out_shape=[jax.ShapeDtypeStruct(*o) for o in outs]...  73.5 us
    convert_element_type x3, local copies, waits for them, and re-layouts, block_grads(): scores = scores + bias.astype(F32)  11.6 us
    unnamed x89, local copies, waits for them, and re-layouts  10.6 us
    dot_general x1, matrix products, block_grads(): jnp.einsum('eahts,eathd->eashd', probs_b, d_att, preferred_element_type=F32)  4.83 us
    dot_general x1, matrix products, block_grads(): jnp.einsum('eahts,eashd->eathd', probs_b, value_rows, preferred_element_t...  4.15 us
    convert_element_type x2, local copies, waits for them, and re-layouts, block_grads(): window_cells = cells.astype(F32)  4.09 us
    convert_element_type x1, local copies, waits for them, and re-layouts, block_grads(): d_score_b = d_score.astype(BF16)  3.96 us
    reshape x1, local copies, waits for them, and re-layouts, block_grads(): packed.reshape(lon_windows, positions, WIN, 3, head_count, head_size)  3.85 us

profile of v2, /device:TPU:0, one launch (start us, length us, event | category | flops | bytes accessed | tf_op | source)
XLA Modules:
  0.0 184.5 jit_solution(17979378072948848808)
XLA Ops:
  10.6 1.6 constant_dynamic-slice_fusion.3
  13.9 32.7 %shard_map.153 = (bf16[8,2,104,192]{3,2,1,0:T(8,128)(2,1)S(1)}, bf16[8,2,24,384]{3,2,1,0:T(8,128)(2,1)S(1)}, bf16[8,24,2592]{2,1,0:T(8,128)(2,1)S(1)}, bf16[288,...) custom-call(bf16[2,104,192]{2,1,0:T(8,128)(2,1)S(1)} %pad_maximum_fusion.7.a, ...), custom_call_target="tpu_custom_call" | custom-call | tf_op jit(solution)/shard_map/pallas_call | solution.py:197
  48.2 1.4 maximum_maximum_fusion
  49.6 1.1 fusion.49
  50.7 2.0 %reshape.416 = f32[576,192]{1,0:T(8,128)} reshape(f32[1,8,6,12,192]{4,3,2,1,0:T(8,128)} %get-tuple-element.59) | data formatting | bytes 884736 | tf_op jit(solution)/shard_map/convert_element_type | solution.py:234
  52.7 2.1 %copy.65 = f32[576,192]{0,1:T(8,128)} copy(f32[576,192]{1,0:T(8,128)} %reshape.416) | data formatting | bytes 884736 | tf_op jit(solution)/shard_map/convert_element_type | solution.py:234
  58.0 1.0 multiply_convert_fusion.1
  59.0 1.1 convert_element_type.139
  61.4 1.2 copy.57
  62.6 3.8 %reshape.399 = bf16[1,4,144,3,6,32]{2,1,5,4,3,0:T(4,128)(2,1)} reshape(bf16[576,576]{0,1:T(8,128)(2,1)} %copy.57) | data formatting | bytes 1327104 | tf_op jit(solution)/shard_map/reshape | solution.py:238
  66.5 2.5 %fusion.48 = (bf16[1,4,144,1,6,32]{2,1,5,4,3,0:T(4,128)(2,1)S(1)}, bf16[1,4,144,1,6,32]{2,1,5,4,3,0:T(4,128)(2,1)S(1)}, bf16[1,4,144,1,6,32]{2,1,5,4,3,0:T(4,128)(2,1)}) fusion(bf16[1,4,144,3,6,32]{2,1,5,4,3,0:T(4,128)(2,1)} %reshape.399), kind=kLoop, calls=%fused_computation.136 | loop fusion | bytes 1327104 | tf_op jit(solution)/shard_map/slice | solution.py:239
  69.1 1.7 copy.61
  70.8 4.3 %reshape.418 = f32[4,6,144,144]{3,2,1,0:T(8,128)} reshape(f32[24,8,2592]{2,1,0:T(8,128)} %copy.61) | data formatting | bytes 3981312 | tf_op jit(solution)/shard_map/convert_element_type | solution.py:241
  75.0 5.6 %copy.62 = f32[4,6,144,144]{2,3,1,0:T(8,128)} copy(f32[4,6,144,144]{3,2,1,0:T(8,128)} %reshape.418) | data formatting | bytes 3981312 | tf_op jit(solution)/shard_map/convert_element_type | solution.py:241
  81.0 2.8 %add_select_fusion = f32[4,6,144,144]{2,3,1,0:T(8,128)S(1)} fusion(f32[4,6,144,144]{2,3,1,0:T(8,128)} %copy.62, pred[4,144,144]{1,2,0:T(8,128)(4,1)S(1)} %broadcast_compare_fusion, bf16[1,4,144,1,6,32]{2,1,5,4,3,0:T(4,128)(2,1)S(1)} %get-tuple-element.56, bf16[1,4,144,1,6,32]{2,1,5,4,3,0:T(4,128)(2,1)S(1)} %get-tuple-element.55), kind=kOutput, calls=%fused_computation.4 | convolution fusion | flops 33343488 | bytes 4506624 | tf_op jit(solution)/shard_map/eathd,eashd->eahts/dot_general | solution.py:240
  83.8 2.8 %fusion.53 = (f32[4,6,144]{2,1,0:T(8,128)S(1)}, f32[4,6,144,144]{2,3,1,0:T(8,128)}) fusion(f32[4,6,144,144]{2,3,1,0:T(8,128)S(1)} %add_select_fusion), kind=kOutput, calls=%fused_computation.141 | output fusion | flops 995471 | bytes 3995136 | tf_op jit(solution)/shard_map/sub | solution.py:244
  86.6 4.1 %fusion.13 = bf16[1,4,144,6,32]{2,4,3,1,0:T(8,128)(2,1)S(1)} fusion(bf16[1,4,144,1,6,32]{2,1,5,4,3,0:T(4,128)(2,1)S(1)} %copy-done.30, f32[4,6,144]{2,1,0:T(8,128)S(1)} %get-tuple-element.75, f32[4,6,144,144]{2,3,1,0:T(8,128)} %copy-done.9), kind=kOutput, calls=%fused_computation.32 | convolution fusion | flops 33457680 | bytes 2446848 | tf_op jit(solution)/shard_map/eahts,eashd->eathd/dot_general | solution.py:247
  92.5 2.2 %fusion.10 = (bf16[768,576]{0,1:T(8,128)(2,1)}, f32[576,768]{1,0:T(8,128)}) fusion(bf16[768,192]{1,0:T(8,128)(2,1)S(1)} %bitcast.189, f32[576,192]{0,1:T(8,128)S(1)} %get-tuple-element.78, f32[192]{0:T(256)S(1)} %reshape.419, f32[576]{0:T(1024)S(1)} %add_rsqrt_fusion.1, f32[576]{0:T(1024)S(1)} %broadcast_multiply_fusion.5), kind=kOutput, calls=%fused_computation.20 | convolution fusion | flops 172523520 | bytes 3396864 | tf_op jit(solution)/shard_map/dot_general | solution.py:229
  95.1 2.4 %fusion.6 = bf16[576,768]{1,0:T(8,128)(2,1)S(1)} fusion(f32[576,768]{1,0:T(8,128)} %get-tuple-element.84, bf16[576,192]{1,0:T(8,128)(2,1)S(1)} %reshape_transpose_reshape_squeeze.4, bf16[192,768]{1,0:T(8,128)(2,1)S(1)} %bitcast.201), kind=kOutput, calls=%fused_computation.13 | convolution fusion | flops 174292992 | bytes 3170304 | tf_op jit(solution)/shard_map/dot_general | solution.py:256
  98.6 1.0 convolution_convert_fusion.5
  99.6 1.2 reshape.405
  100.8 4.8 %convolution_bitcast_fusion = bf16[1,4,144,1,6,32]{2,5,4,1,3,0:T(8,128)(2,1)} fusion(bf16[4,144,6,32]{1,0,3,2:T(4,128)(2,1)S(1)} %reshape.405, f32[4,6,144]{2,1,0:T(8,128)S(1)} %get-tuple-element.75, f32[4,6,144,144]{2,3,1,0:T(8,128)} %copy-done.9), kind=kOutput, calls=%fused_computation.22 | convolution fusion | flops 33347088 | bytes 2446848 | tf_op jit(solution)/shard_map/eahts,eathd->eashd/dot_general | solution.py:266
  105.7 2.9 %multiply_reduce_fusion = (f32[4,6,144]{2,1,0:T(8,128)S(1)}, f32[4,6,144,144]{2,3,1,0:T(8,128)S(1)}) fusion(f32[4,6,144,144]{2,3,1,0:T(8,128)} %get-tuple-element.76, f32[4,6,144]{2,1,0:T(8,128)S(1)} %get-tuple-element.75, bf16[1,4,144,1,6,32]{2,1,5,4,3,0:T(4,128)(2,1)S(1)} %copy-done.31, bf16[4,144,6,32]{1,0,3,2:T(4,128)(2,1)S(1)} %reshape.405), kind=kOutput, calls=%fused_computation.2 | convolution fusion | flops 33340032 | bytes 4451328 | tf_op jit(solution)/shard_map/eathd,eashd->eahts/dot_general | solution.py:265
  111.7 1.0 copy.73
  112.7 1.6 convert_element_type.157
  114.4 1.9 %multiply_reduce_fusion.4 = (bf16[192]{0:T(256)(128)(2,1)S(1)}, f32[576]{0:T(1024)S(1)}, f32[576]{0:T(1024)S(1)}, f32[576,192]{0,1:T(8,128)S(1)}) fusion(f32[576,192]{0,1:T(8,128)S(1)} %copy-done.10, f32[576]{0:T(1024)S(1)} %copy-done.35, f32[576]{0:T(1024)S(1)} %copy-done.36, f32[192]{0:T(256)S(1)} %copy-done.39, ...), kind=kOutput, calls=%fused_computation.58 | convolution fusion | flops 128285376 | bytes 1779840 | tf_op jit(solution)/shard_map/dot_general | solution.py:273
  121.3 4.0 %copy.81 = bf16[4,6,144,144]{3,2,1,0:T(8,128)(2,1)} copy(bf16[4,6,144,144]{2,3,1,0:T(8,128)(2,1)} %copy-done.7) | data formatting | bytes 1990656 | tf_op jit(solution)/shard_map/convert_element_type | solution.py:268
  125.3 3.0 %convert_element_type.161 = bf16[24,8,2592]{2,1,0:T(8,128)(2,1)S(1)} reshape(bf16[4,6,144,144]{3,2,1,0:T(8,128)(2,1)} %copy.81) | data formatting | bytes 1990656 | tf_op jit(solution)/shard_map/convert_element_type | solution.py:345
  131.2 40.8 %shard_map.154 = (f32[2,104,192]{2,1,0:T(8,128)S(1)}, f32[2,24,384]{2,1,0:T(8,128)S(1)}, f32[96,2592]{1,0:T(8,128)S(1)}, bf16[144,192]{1,0:T(8,128)(2,1)S(1)}, b...) custom-call(bf16[2,8,104,192]{3,2,1,0:T(8,128)(2,1)S(1)} %pad_maximum_fusion.a, ...), custom_call_target="tpu_custom_call" | custom-call | tf_op jit(solution)/shard_map/pallas_call | solution.py:197
  175.2 1.0 reshape.413
  178.0 1.1 fusion.28
  183.3 1.1 copy.89
  (179 shorter events, 35.2 us)
Async XLA Ops:
  0.6 11.7 %copy-start.33 = (bf16[8,6,12,192]{3,0,2,1:T(8,128)(2,1)S(1)}, bf16[8,6,12,192]{3,0,2,1:T(8,128)(2,1)}, u32[]{:S(2)}) copy-start(bf16[8,6,12,192]{3,0,2,1:T(8,128)(2,1)} %param.11) | copy-start | bytes 663556
  0.6 11.7 %copy-start.34 = (bf16[8,6,12,192]{3,0,2,1:T(8,128)(2,1)S(1)}, bf16[8,6,12,192]{3,0,2,1:T(8,128)(2,1)}, u32[]{:S(2)}) copy-start(bf16[8,6,12,192]{3,0,2,1:T(8,128)(2,1)} %param.10) | copy-start | bytes 663556
  60.2 2.4 %copy-start.23 = (bf16[576,192]{1,0:T(8,128)(2,1)}, bf16[576,192]{1,0:T(8,128)(2,1)S(1)}, u32[]{:S(2)}) copy-start(bf16[576,192]{1,0:T(8,128)(2,1)S(1)} %convert_element_type.139) | copy-start | bytes 663556
  68.9 12.0 %copy-start.11 = (bf16[1,4,144,1,6,32]{2,1,5,4,3,0:T(4,128)(2,1)}, bf16[1,4,144,1,6,32]{2,1,5,4,3,0:T(4,128)(2,1)S(1)}, u32[]{:S(2)}) copy-start(bf16[1,4,144,1,6,32]{2,1,5,4,3,0:T(4,128)(2,1)S(1)} %get-tuple-element.56) | copy-start | bytes 663556
  75.0 5.6 %copy-start.41 = (s32[8,6]{1,0:T(8,128)S(1)}, s32[8,6]{1,0:T(8,128)}, u32[]{:S(2)}) copy-start(s32[8,6]{1,0:T(8,128)} %param.19) | copy-start | bytes 580
  83.8 2.8 %copy-start.9 = (f32[4,6,144,144]{2,3,1,0:T(8,128)}, f32[4,6,144,144]{2,3,1,0:T(8,128)S(1)}, u32[]{:S(2)}) copy-start(f32[4,6,144,144]{2,3,1,0:T(8,128)S(1)} %add_select_fusion) | copy-start | bytes 5971972
  83.8 2.8 %copy-start.30 = (bf16[1,4,144,1,6,32]{2,1,5,4,3,0:T(4,128)(2,1)S(1)}, bf16[1,4,144,1,6,32]{2,1,5,4,3,0:T(4,128)(2,1)}, u32[]{:S(2)}) copy-start(bf16[1,4,144,1,6,32]{2,1,5,4,3,0:T(4,128)(2,1)} %get-tuple-element.57) | copy-start | bytes 663556
  86.6 5.5 %copy-start.10 = (f32[576,192]{0,1:T(8,128)S(1)}, f32[576,192]{0,1:T(8,128)}, u32[]{:S(2)}) copy-start(f32[576,192]{0,1:T(8,128)} %copy.65) | copy-start | bytes 1327108
  90.7 1.7 copy-start.37
  92.5 2.2 %copy-start.17 = (bf16[8,1,96,192]{3,2,1,0:T(8,128)(2,1)}, bf16[8,1,96,192]{3,2,1,0:T(8,128)(2,1)S(1)}, u32[]{:S(2)}) copy-start(bf16[8,1,96,192]{3,2,1,0:T(8,128)(2,1)S(1)} %slice.124) | copy-start | bytes 884740
  92.5 2.2 %copy-start.27 = (bf16[1,8,6,12,192]{4,3,2,1,0:T(8,128)(2,1)S(1)}, bf16[1,8,6,12,192]{4,3,2,1,0:T(8,128)(2,1)}, u32[]{:S(2)}) copy-start(bf16[1,8,6,12,192]{4,3,2,1,0:T(8,128)(2,1)} %get-tuple-element.58) | copy-start | bytes 663556
  94.8 3.4 %copy-start.21 = (bf16[576,192]{1,0:T(8,128)(2,1)}, bf16[576,192]{1,0:T(8,128)(2,1)S(1)}, u32[]{:S(2)}) copy-start(bf16[576,192]{1,0:T(8,128)(2,1)S(1)} %reshape_transpose_reshape_squeeze.4) | copy-start | bytes 663556
  95.1 2.4 %copy-start.18 = (bf16[8,1,96,192]{3,2,1,0:T(8,128)(2,1)S(1)}, bf16[8,1,96,192]{3,2,1,0:T(8,128)(2,1)}, u32[]{:S(2)}) copy-start(bf16[8,1,96,192]{3,2,1,0:T(8,128)(2,1)} %copy-done.17) | copy-start | bytes 884740
  97.5 1.1 copy-start.13
  98.6 7.1 %copy-start.25 = (bf16[576,192]{0,1:T(8,128)(2,1)}, bf16[576,192]{0,1:T(8,128)(2,1)S(1)}, u32[]{:S(2)}) copy-start(bf16[576,192]{0,1:T(8,128)(2,1)S(1)} %fusion.46) | copy-start | bytes 663556
  100.8 4.8 %copy-start.31 = (bf16[1,4,144,1,6,32]{2,1,5,4,3,0:T(4,128)(2,1)S(1)}, bf16[1,4,144,1,6,32]{2,1,5,4,3,0:T(4,128)(2,1)}, u32[]{:S(2)}) copy-start(bf16[1,4,144,1,6,32]{2,1,5,4,3,0:T(4,128)(2,1)} %get-tuple-element.57) | copy-start | bytes 663556
  105.7 3.1 %copy-start.8 = (f32[4,6,144,144]{2,3,1,0:T(8,128)S(1)}, f32[4,6,144,144]{2,3,1,0:T(8,128)}, u32[]{:S(2)}) copy-start(f32[4,6,144,144]{2,3,1,0:T(8,128)} %get-tuple-element.76) | copy-start | bytes 5971972
  109.7 1.2 copy-start.7
  110.4 1.0 copy-start.32
  111.6 2.7 %copy-start.29 = (bf16[8,1,72,192]{3,2,1,0:T(8,128)(2,1)S(1)}, bf16[8,1,72,192]{3,2,1,0:T(8,128)(2,1)}, u32[]{:S(2)}) copy-start(bf16[8,1,72,192]{3,2,1,0:T(8,128)(2,1)} %copy-done.28) | copy-start | bytes 663556
  111.7 2.7 %copy-start.35 = (f32[576]{0:T(1024)S(1)}, f32[576]{0:T(1024)}, u32[]{:S(2)}) copy-start(f32[576]{0:T(1024)} %rsqrt.22) | copy-start | bytes 6916
  111.7 2.7 %copy-start.36 = (f32[576]{0:T(1024)S(1)}, f32[576]{0:T(1024)}, u32[]{:S(2)}) copy-start(f32[576]{0:T(1024)} %div.43) | copy-start | bytes 6916
  111.7 2.7 %copy-start.39 = (f32[192]{0:T(256)S(1)}, f32[192]{0:T(256)}, u32[]{:S(2)}) copy-start(f32[192]{0:T(256)} %copy-done.38) | copy-start | bytes 2308
  116.3 1.4 copy-start.16
  116.7 1.3 copy-start.26
  116.7 1.6 copy-start.20
  116.7 1.6 copy-start.24
  117.7 1.2 copy-start.14
  119.4 1.3 copy-start.19
  125.3 3.1 %copy-start.40 = (s32[4,4]{1,0:T(4,128)S(1)}, s32[4,4]{1,0:T(4,128)}, u32[]{:S(2)}) copy-start(s32[4,4]{1,0:T(4,128)} %param.18) | copy-start | bytes 196
  175.2 4.8 %copy-start.1 = (f32[2,104,192]{2,1,0:T(8,128)S(1)}, f32[2,104,192]{2,1,0:T(8,128)}, u32[]{:S(2)}) copy-start(f32[2,104,192]{2,1,0:T(8,128)} %copy-done) | copy-start | bytes 479236
  175.2 6.8 %copy-start.3 = (f32[2,24,384]{2,1,0:T(8,128)S(1)}, f32[2,24,384]{2,1,0:T(8,128)}, u32[]{:S(2)}) copy-start(f32[2,24,384]{2,1,0:T(8,128)} %copy-done.2) | copy-start | bytes 221188
  (10 other events, 7.2 us)

commit v3 on v2

--- a/solution.py
+++ b/solution.py
@@ -217,65 +217,109 @@
     return shaped.transpose(1, 3, 2, 4, 0, 5, 6).reshape(p, l, c, flat.shape[-1])
 
 
+def by_t(x, w_t):
+    return lax.dot_general(x, w_t, (((1,), (1,)), ((), ())), preferred_element_type=F32)
+
+
+def outer(x, y):
+    return lax.dot_general(x, y, (((0,), (0,)), ((), ())), preferred_element_type=F32)
+
+
+def plain(x, y):
+    return jnp.dot(x, y, preferred_element_type=F32)
+
+
+def window_kernel(cells, cots, qkv_t, proj_t, up_t, down_t, gains, bias, label_col, label_row,
+                  d_cells, g_qkv, g_proj, g_up, g_down, g_gain, table, probs_s):
+    positions, head_count = bias.shape[:2]
+    windows, _, features = cells.shape
+    head_size = features // head_count
+    factor = 1.0 / math.sqrt(head_size)
+    for total in (g_qkv, g_proj, g_up, g_down, g_gain):
+        total[...] = jnp.zeros(total.shape, F32)
+    if windows > positions:
+        table[...] = jnp.zeros(table.shape, F32)
+
+    def body(w, carry):
+        p = lax.rem(w, positions)
+        gain_one, gain_two = gains[0:1].astype(F32), gains[1:2].astype(F32)
+        lane_head = lax.broadcasted_iota(jnp.int32, (1, features), 1) // head_size
+        heads = [(lane_head == h).astype(BF16) for h in range(head_count)]
+        normed_one, inv_one = layer_norm(cells[w].astype(F32))
+        scaled_one = (normed_one * gain_one).astype(BF16)
+        q, k, v = (
+            by_t(scaled_one, qkv_t[i * features : (i + 1) * features]).astype(BF16) for i in range(3)
+        )
+        same = label_col[p] == label_row[p]
+        attended = jnp.zeros((WIN, features), F32)
+        for h, head in enumerate(heads):
+            scores = by_t(q * head, k) * factor + bias[p, h].astype(F32)
+            scores = jnp.where(same, scores, -jnp.inf)
+            raised = jnp.exp(scores - jnp.max(scores, axis=-1, keepdims=True))
+            probs = raised * (1.0 / jnp.sum(raised, axis=-1, keepdims=True))
+            probs_s[h] = probs
+            attended = attended + plain(probs.astype(BF16), v * head)
+        attended = attended.astype(BF16)
+        middle = cells[w].astype(F32) + by_t(attended, proj_t[...])
+        normed_two, inv_two = layer_norm(middle)
+        scaled_two = (normed_two * gain_two).astype(BF16)
+        cot = cots[w]
+        activated, slope = gelu_pair(by_t(scaled_two, up_t[...]))
+        g_down[...] += outer(cot, activated.astype(BF16))
+        d_hidden = (plain(cot, down_t[...]) * slope).astype(BF16)
+        g_up[...] += outer(d_hidden, scaled_two)
+        d_htwo = plain(d_hidden, up_t[...])
+        g_gain[1:2] += jnp.sum(d_htwo * normed_two, axis=0, keepdims=True)
+        d_middle = cot.astype(F32) + norm_back(d_htwo * gain_two, normed_two, inv_two)
+        d_middle_b = d_middle.astype(BF16)
+        g_proj[...] += outer(d_middle_b, attended)
+        d_att = plain(d_middle_b, proj_t[...]).astype(BF16)
+        d_q, d_k, d_v = (jnp.zeros((WIN, features), F32) for _ in range(3))
+        for h, head in enumerate(heads):
+            probs, d_att_h = probs_s[h], d_att * head
+            d_prob = by_t(d_att_h, v)
+            d_v = d_v + outer(probs.astype(BF16), d_att_h)
+            d_score = probs * (d_prob - jnp.sum(probs * d_prob, axis=-1, keepdims=True))
+            if windows > positions:
+                table[p, h] += d_score
+            else:
+                table[p, h] = d_score.astype(table.dtype)
+            d_score_b = d_score.astype(BF16)
+            d_q = d_q + plain(d_score_b, k * head)
+            d_k = d_k + outer(d_score_b, q * head)
+        d_hone = jnp.zeros((WIN, features), F32)
+        for i, part in enumerate((d_q * factor, d_k * factor, d_v)):
+            part = part.astype(BF16)
+            span = slice(i * features, (i + 1) * features)
+            g_qkv[span] += outer(part, scaled_one)
+            d_hone = d_hone + plain(part, qkv_t[span])
+        g_gain[0:1] += jnp.sum(d_hone * normed_one, axis=0, keepdims=True)
+        d_cells[w] = (d_middle + norm_back(d_hone * gain_one, normed_one, inv_one)).astype(BF16)
+        return carry
+
+    lax.fori_loop(0, windows, body, 0)
+
+
 def block_grads(cells, cots, qkv_t, proj_t, up_t, down_t, gains, bias, labels):
     features = cells.shape[1]
     positions, head_count = bias.shape[:2]
-    head_size = features // head_count
-    lon_windows = cells.shape[0] // (positions * WIN)
-    factor = 1.0 / math.sqrt(head_size)
-    gain_one, gain_two = gains[0].astype(F32), gains[1].astype(F32)
-
-    def by_t(x, w_t):
-        return lax.dot_general(x, w_t, (((1,), (1,)), ((), ())), preferred_element_type=F32)
-
-    def outer(x, y):
-        return lax.dot_general(x, y, (((0,), (0,)), ((), ())), preferred_element_type=F32)
-
-    window_cells = cells.astype(F32)
-    normed_one, inv_one = layer_norm(window_cells)
-    scaled_one = (normed_one * gain_one).astype(BF16)
-    packed = by_t(scaled_one, qkv_t).astype(BF16)
-    packed = packed.reshape(lon_windows, positions, WIN, 3, head_count, head_size)
-    queries, key_rows, value_rows = packed[:, :, :, 0], packed[:, :, :, 1], packed[:, :, :, 2]
-    scores = jnp.einsum("eathd,eashd->eahts", queries, key_rows, preferred_element_type=F32) * factor
-    scores = scores + bias.astype(F32)
-    same = labels[:, None, :, None] == labels[:, None, None, :]
-    scores = jnp.where(same, scores, -jnp.inf)
-    raised = jnp.exp(scores - jnp.max(scores, axis=-1, keepdims=True))
-    probs = raised / jnp.sum(raised, axis=-1, keepdims=True)
-    probs_b = probs.astype(BF16)
-    attended = jnp.einsum("eahts,eashd->eathd", probs_b, value_rows, preferred_element_type=F32)
-    attended = attended.astype(BF16).reshape(-1, features)
-    middle = window_cells + by_t(attended, proj_t)
-    normed_two, inv_two = layer_norm(middle)
-    scaled_two = (normed_two * gain_two).astype(BF16)
-    pre_act = by_t(scaled_two, up_t)
-    activated, slope = gelu_pair(pre_act)
-    hidden_b = activated.astype(BF16)
-    g_down_t = outer(cots, hidden_b)
-    d_hidden = (jnp.dot(cots, down_t, preferred_element_type=F32) * slope).astype(BF16)
-    g_up_t = outer(d_hidden, scaled_two)
-    d_htwo = jnp.dot(d_hidden, up_t, preferred_element_type=F32)
-    g_gain_two = jnp.sum(d_htwo * normed_two, axis=0)
-    d_middle = cots.astype(F32) + norm_back(d_htwo * gain_two, normed_two, inv_two)
-    d_middle_b = d_middle.astype(BF16)
-    g_proj_t = outer(d_middle_b, attended)
-    d_att = jnp.dot(d_middle_b, proj_t, preferred_element_type=F32).astype(BF16)
-    d_att = d_att.reshape(lon_windows, positions, WIN, head_count, head_size)
-    d_prob = jnp.einsum("eathd,eashd->eahts", d_att, value_rows, preferred_element_type=F32)
-    d_values = jnp.einsum("eahts,eathd->eashd", probs_b, d_att, preferred_element_type=F32)
-    d_score = probs * (d_prob - jnp.sum(probs * d_prob, axis=-1, keepdims=True))
-    d_score_b = d_score.astype(BF16)
-    d_queries = jnp.einsum("eahts,eashd->eathd", d_score_b, key_rows, preferred_element_type=F32) * factor
-    d_keys = jnp.einsum("eahts,eathd->eashd", d_score_b, queries, preferred_element_type=F32) * factor
-    d_packed = jnp.stack([d_queries, d_keys, d_values], axis=3).astype(BF16).reshape(-1, 3 * features)
-    g_qkv_t = outer(d_packed, scaled_one)
-    d_hone = jnp.dot(d_packed, qkv_t, preferred_element_type=F32)
-    g_gain_one = jnp.sum(d_hone * normed_one, axis=0)
-    d_cells = d_middle + norm_back(d_hone * gain_one, normed_one, inv_one)
-    table = jnp.sum(d_score, axis=0)
-    gains_grad = jnp.stack([g_gain_one, g_gain_two])
-    return d_cells.astype(BF16), g_qkv_t, g_proj_t, g_up_t, g_down_t, gains_grad, table
+    windows = cells.shape[0] // WIN
+    vmem = pl.BlockSpec(memory_space=pltpu.VMEM)
+    outs = [((windows, WIN, features), BF16)]
+    outs += [(w.shape, F32) for w in (qkv_t, proj_t, up_t, down_t)] + [((2, features), F32)]
+    outs += [(bias.shape, F32 if windows > positions else BF16)]
+    d_cells, *grads = pl.pallas_call(
+        window_kernel,
+        out_shape=[jax.ShapeDtypeStruct(*o) for o in outs],
+        in_specs=[vmem] * 10,
+        out_specs=[vmem] * len(outs),
+        scratch_shapes=[pltpu.VMEM((head_count, WIN, WIN), F32)],
+        compiler_params=pltpu.CompilerParams(vmem_limit_bytes=48 * 2**20),
+    )(
+        cells.reshape(windows, WIN, features), cots.reshape(windows, WIN, features),
+        qkv_t, proj_t, up_t, down_t, gains, bias, labels[:, :, None], labels[:, None, :],
+    )
+    return (d_cells.reshape(cells.shape), *grads)
 
 
 def shards(inputs, cotangent, qkv_weight, proj_weight, up_weight, down_weight, norm_gains, bias_table, type_of, region):

time: 186 us -> 131 us (0.70)
  local copies, waits for them, and re-layouts: 65.2 us -> 28.6 us
  matrix products: 26 us -> 0 us
  Pallas kernels: 73.5 us -> 92.5 us
  other arithmetic: 12.4 us -> 2.56 us
    convert_element_type x16 -> x2, local copies, waits for them, and re-layouts: 28.3 us -> 0.11 us  [shards(): g_down_t.reshape(nlon, -1, 2, g_down_t.shape[1] // 2).transpose(2, 0, 1, 3)]
    dot_general x17 -> x0, matrix products: 26 us -> none  [the longest x1 4.83 us: block_grads(): jnp.einsum('eahts,eathd->eashd', probs_b, d_att, preferred_element_type=F32)]
    pallas_call x0 -> x1, Pallas kernels: none -> 19 us  [block_grads(): pl.pallas_call(window_kernel, out_shape=[jax.ShapeDtypeStruct(*o) for o i...]
    convert_element_type x7 -> x1, other arithmetic: 3.47 us -> 0.03 us  [shards(): g_down_t.reshape(nlon, -1, 2, g_down_t.shape[1] // 2).transpose(2, 0, 1, 3)]
    sub x1 -> x0, other arithmetic: 2.79 us -> none  [block_grads(): raised = jnp.exp(scores - jnp.max(scores, axis=-1, keepdims=True))]
    slice x1, local copies, waits for them, and re-layouts: 2.48 us -> 0.06 us  [shards(): shifted[1]]
    reshape x3 -> x6, local copies, waits for them, and re-layouts: 4.34 us -> 6.29 us  [the longest x2 3.66 us: shards(): table.astype(BF16).reshape(positions * head_count, nlon, part)]
    unnamed x89 -> x59, local copies, waits for them, and re-layouts: 10.6 us -> 10.7 us
where the time goes in v3:
time: 131 us
  Pallas kernels  92.5 us (71%)
  local copies, waits for them, and re-layouts  28.6 us (22%)
  between operations  7.1 us (5%)
  other arithmetic  2.56 us (2%)
    pallas_call x2, Pallas kernels, comm_call(): pl.pallas_call(kernel, out_shape=[jax.ShapeDtypeStruct(*o) for o in outs]...  73.5 us
    pallas_call x1, Pallas kernels, block_grads(): pl.pallas_call(window_kernel, out_shape=[jax.ShapeDtypeStruct(*o) for o i...  19 us
    unnamed x59, local copies, waits for them, and re-layouts  10.7 us
    reshape x2, local copies, waits for them, and re-layouts, shards(): table.astype(BF16).reshape(positions * head_count, nlon, part)  3.66 us

profile of v3, /device:TPU:0, one launch (start us, length us, event | category | flops | bytes accessed | tf_op | source)
XLA Modules:
  0.0 130.7 jit_solution(903403823350930780)
XLA Ops:
  0.6 0.9 fusion.21
  1.5 0.5 fusion.25
  8.0 1.6 %constant_dynamic-slice_fusion.3 = (bf16[1,6,2592]{2,0,1:T(2,128)(2,1)S(1)}, bf16[1,6,2592]{2,0,1:T(2,128)(2,1)S(1)}, bf16[1,6,2592]{2,0,1:T(2,128)(2,1)S(1)}, bf16[1,6,2592]{2,0,1:T(2,128)(2,1)S(1)}) fusion(bf16[16,6,2592]{2,0,1:T(8,128)(2,1)} %param.17, s32[]{:T(128)S(6)} %select_n.18, s32[]{:T(128)S(6)} %select_n.20, s32[]{:T(128)S(6)} %select_n.19, ...), kind=kLoop, calls=%fused_computation.56 | loop fusion | bytes 248848 | tf_op jit(solution)/shard_map/jit(dynamic_index_in_dim)/dynamic_slice | solution.py:348
  9.7 1.2 copy_bitcast_fusion.1
  12.3 32.7 %shard_map.153 = (bf16[8,2,104,192]{3,2,1,0:T(8,128)(2,1)S(1)}, bf16[8,2,24,384]{3,2,1,0:T(8,128)(2,1)S(1)}, bf16[8,24,2592]{2,1,0:T(8,128)(2,1)S(1)}, bf16[288,...) custom-call(bf16[2,104,192]{2,1,0:T(8,128)(2,1)S(1)} %pad_maximum_fusion.7.a, ...), custom_call_target="tpu_custom_call" | custom-call | tf_op jit(solution)/shard_map/pallas_call | solution.py:197
  45.1 2.4 %reshape.132.bias = bf16[4,6,144,144]{3,2,1,0:T(8,128)(2,1)} reshape(bf16[24,8,2592]{2,1,0:T(8,128)(2,1)S(1)} %copy.46) | data formatting | bytes 1990656 | tf_op jit(solution)/shard_map/reshape | solution.py:368
  48.3 0.9 reshape_reshape_transpose_reshape_squeeze.7.cots
  49.5 0.6 slice.100
  50.5 1.0 copy-done
  51.5 0.9 copy-done.4
  52.4 19.0 %shard_map.154 = (bf16[4,144,192]{2,1,0:T(8,128)(2,1)S(1)}, f32[576,192]{1,0:T(8,128)S(1)}, f32[192,192]{1,0:T(8,128)S(1)}, f32[768,192]{1,0:T(8,128)S(1)}, f32[...) custom-call(bf16[4,144,192]{2,1,0:T(8,128)(2,1)S(1)} %reshape_reshape_transpose_reshape_squeeze.6.cell, ...), custom_call_target="tpu_custom_call" | custom-call | tf_op jit(solution)/shard_map/pallas_call | solution.py:311
  71.4 0.7 copy-done.5
  72.1 0.7 copy-done.7
  72.9 0.8 copy-done.1
  74.0 1.1 convert.33
  75.4 2.3 %reshape.137 = bf16[24,8,2592]{2,1,0:T(8,128)(2,1)} reshape(bf16[4,6,144,144]{3,2,1,0:T(8,128)(2,1)S(1)} %get-tuple-element.37) | data formatting | bytes 1990656 | tf_op jit(solution)/shard_map/reshape | solution.py:389
  77.6 1.4 %copy.75 = bf16[24,8,2592]{2,0,1:T(8,128)(2,1)S(1)} copy(bf16[24,8,2592]{2,1,0:T(8,128)(2,1)} %reshape.137) | data formatting | bytes 1990656 | tf_op jit(solution)/shard_map/reshape | solution.py:389
  79.3 0.7 fusion.24
  80.5 0.4 reshape.139
  81.0 40.8 %shard_map.155 = (f32[2,104,192]{2,1,0:T(8,128)S(1)}, f32[2,24,384]{2,1,0:T(8,128)S(1)}, f32[96,2592]{1,0:T(8,128)S(1)}, bf16[144,192]{1,0:T(8,128)(2,1)S(1)}, b...) custom-call(bf16[2,8,104,192]{3,2,1,0:T(8,128)(2,1)S(1)} %pad_maximum_fusion.a, ...), custom_call_target="tpu_custom_call" | custom-call | tf_op jit(solution)/shard_map/pallas_call | solution.py:197
  121.8 0.7 copy-done.9
  122.5 0.6 copy-done.11
  123.1 0.6 copy-done.13
  123.7 0.6 copy-done.15
  124.4 0.6 copy-done.17
  125.2 1.1 copy.57
  126.6 0.9 copy.55
  127.5 0.7 copy.56
  128.3 0.6 copy.63
  128.9 0.6 slice_bitcast_fusion.1
  129.5 0.6 slice_bitcast_fusion.2
  130.2 0.6 slice_bitcast_fusion.4
  (100 shorter events, 4.7 us)
Async XLA Ops:
  11.3 0.8 copy-start.20
  11.3 0.9 copy-start.21
  11.3 0.9 copy-start.23
  11.3 0.9 copy-start.26
  11.3 0.9 copy-start.22
  48.3 2.0 %copy-start.25 = (s32[8,6]{1,0:T(8,128)S(1)}, s32[8,6]{1,0:T(8,128)}, u32[]{:S(2)}) copy-start(s32[8,6]{1,0:T(8,128)} %param.19) | copy-start | bytes 580
  50.5 1.0 copy-start
  51.5 0.9 copy-start.4
  71.4 0.7 copy-start.5
  72.1 0.7 copy-start.7
  72.8 0.8 copy-start.1
  72.8 1.0 copy-start.3
  72.8 2.3 %copy-start.8 = (f32[192,192]{1,0:T(8,128)S(1)}, f32[192,192]{1,0:T(8,128)}, u32[]{:S(2)}) copy-start(f32[192,192]{1,0:T(8,128)} %copy-done.7) | copy-start | bytes 442372
  77.6 1.4 %copy-start.2 = (f32[192,768]{1,0:T(8,128)S(1)}, f32[192,768]{1,0:T(8,128)}, u32[]{:S(2)}) copy-start(f32[192,768]{1,0:T(8,128)} %copy-done.1) | copy-start | bytes 1769476
  77.6 1.6 %copy-start.6 = (bf16[4,144,192]{2,1,0:T(8,128)(2,1)S(1)}, bf16[4,144,192]{2,1,0:T(8,128)(2,1)}, u32[]{:S(2)}) copy-start(bf16[4,144,192]{2,1,0:T(8,128)(2,1)} %copy-done.5) | copy-start | bytes 663556
  79.1 1.1 copy-start.24
  121.8 0.7 copy-start.9
  122.5 0.6 copy-start.11
  123.1 0.6 copy-start.13
  123.7 0.6 copy-start.15
  124.4 0.6 copy-start.17
  125.1 1.2 copy-start.18
  125.1 1.2 copy-start.16
  125.2 1.3 copy-start.14
  125.2 1.3 copy-start.19
  126.3 1.2 copy-start.10
  126.3 1.9 %copy-start.12 = (f32[2,24,384]{2,1,0:T(8,128)S(1)}, f32[2,24,384]{2,1,0:T(8,128)}, u32[]{:S(2)}) copy-start(f32[2,24,384]{2,1,0:T(8,128)} %copy-done.11) | copy-start | bytes 221188

commit v4 on v3

--- a/solution.py
+++ b/solution.py
@@ -229,8 +229,42 @@
     return jnp.dot(x, y, preferred_element_type=F32)
 
 
-def window_kernel(cells, cots, qkv_t, proj_t, up_t, down_t, gains, bias, label_col, label_row,
-                  d_cells, g_qkv, g_proj, g_up, g_down, g_gain, table, probs_s):
+def pick_kernel(types, table, out):
+    positions = types.shape[0]
+    rows = [table[types[i]].astype(F32) for i in range(positions)]
+    out[...] = jnp.concatenate(rows, axis=0).astype(BF16)
+
+
+def pick_rows(types, table):
+    _, head_count, part = table.shape
+    return pl.pallas_call(
+        pick_kernel,
+        out_shape=jax.ShapeDtypeStruct((types.shape[0] * head_count, part), BF16),
+        in_specs=[pl.BlockSpec(memory_space=pltpu.SMEM), pl.BlockSpec(memory_space=pltpu.VMEM)],
+        out_specs=pl.BlockSpec(memory_space=pltpu.VMEM),
+    )(types, table)
+
+
+def window_kernel(n_up, n_qkv, n_proj, cells, cots, a_all, d_all, bias, label_col, label_row,
+                  d_cells, ga, gd, table,
+                  probs_s, qkv_t, proj_t, up_t, down_t, gains, g_qkv, g_proj, g_up, g_down, g_gain):
+    owners, height = a_all.shape[0], a_all.shape[2]
+
+    def joined(half, start, count):
+        rows = [a_all[j, half].astype(F32)[start : start + count] for j in range(owners)]
+        return jnp.concatenate(rows, axis=0).astype(BF16)
+
+    up_t[...] = joined(0, 0, n_up)
+    qkv_t[...] = joined(1, 0, n_qkv)
+    proj_t[...] = joined(1, n_qkv, n_proj)
+    wide = d_all.shape[3]
+    for i in range(2):
+        rows = [d_all[j, i].astype(F32) for j in range(owners)]
+        down_t[:, i * wide : (i + 1) * wide] = jnp.concatenate(rows, axis=0).astype(BF16)
+    gain_sum = a_all[0, 0].astype(F32)[n_up : n_up + 2]
+    for j in range(1, owners):
+        gain_sum = gain_sum + a_all[j, 0].astype(F32)[n_up : n_up + 2]
+    gains[...] = gain_sum
     positions, head_count = bias.shape[:2]
     windows, _, features = cells.shape
     head_size = features // head_count
@@ -242,7 +276,7 @@
 
     def body(w, carry):
         p = lax.rem(w, positions)
-        gain_one, gain_two = gains[0:1].astype(F32), gains[1:2].astype(F32)
+        gain_one, gain_two = gains[0:1], gains[1:2]
         lane_head = lax.broadcasted_iota(jnp.int32, (1, features), 1) // head_size
         heads = [(lane_head == h).astype(BF16) for h in range(head_count)]
         normed_one, inv_one = layer_norm(cells[w].astype(F32))
@@ -298,26 +332,41 @@
         return carry
 
     lax.fori_loop(0, windows, body, 0)
-
-
-def block_grads(cells, cots, qkv_t, proj_t, up_t, down_t, gains, bias, labels):
+    features = cells.shape[2]
+    down = d_all.shape[2]
+    gain_rows = jnp.concatenate([g_gain[...], jnp.zeros((height - n_up - 2, features), F32)], axis=0)
+    spare = height - n_qkv - n_proj
+    for j in range(owners):
+        ga[0, j] = jnp.concatenate([g_up[j * n_up : (j + 1) * n_up], gain_rows], axis=0).astype(BF16)
+        rows = [g_qkv[j * n_qkv : (j + 1) * n_qkv], g_proj[j * n_proj : (j + 1) * n_proj]]
+        rows += [jnp.zeros((spare, features), F32)] if spare else []
+        ga[1, j] = jnp.concatenate(rows, axis=0).astype(BF16)
+        for i in range(2):
+            gd[i, j] = g_down[j * down : (j + 1) * down, i * wide : (i + 1) * wide].astype(BF16)
+
+
+def block_grads(cells, cots, a_all, d_all, cuts, bias, labels):
     features = cells.shape[1]
     positions, head_count = bias.shape[:2]
-    windows = cells.shape[0] // WIN
+    windows, owners, wide = cells.shape[0] // WIN, a_all.shape[0], d_all.shape[3] * 2
     vmem = pl.BlockSpec(memory_space=pltpu.VMEM)
     outs = [((windows, WIN, features), BF16)]
-    outs += [(w.shape, F32) for w in (qkv_t, proj_t, up_t, down_t)] + [((2, features), F32)]
+    outs += [((2, owners) + x.shape[2:], BF16) for x in (a_all, d_all)]
     outs += [(bias.shape, F32 if windows > positions else BF16)]
+    n_up, n_qkv, n_proj = cuts
+    sizes = [(owners * n, features) for n in (n_qkv, n_proj, n_up)] + [(features, wide)]
     d_cells, *grads = pl.pallas_call(
-        window_kernel,
+        functools.partial(window_kernel, *cuts),
         out_shape=[jax.ShapeDtypeStruct(*o) for o in outs],
-        in_specs=[vmem] * 10,
+        in_specs=[vmem] * 7,
         out_specs=[vmem] * len(outs),
-        scratch_shapes=[pltpu.VMEM((head_count, WIN, WIN), F32)],
+        scratch_shapes=[pltpu.VMEM((head_count, WIN, WIN), F32)]
+        + [pltpu.VMEM(size, BF16) for size in sizes] + [pltpu.VMEM((2, features), F32)]
+        + [pltpu.VMEM(size, F32) for size in sizes] + [pltpu.VMEM((2, features), F32)],
         compiler_params=pltpu.CompilerParams(vmem_limit_bytes=48 * 2**20),
     )(
         cells.reshape(windows, WIN, features), cots.reshape(windows, WIN, features),
-        qkv_t, proj_t, up_t, down_t, gains, bias, labels[:, :, None], labels[:, None, :],
+        a_all, d_all, bias, labels[:, :, None], labels[:, None, :],
     )
     return (d_cells.reshape(cells.shape), *grads)
 
@@ -334,7 +383,10 @@
     types = lax.dynamic_index_in_dim(all_types, lat_index, 0, keepdims=False)
     n_up, n_qkv, n_proj = up_weight.shape[1], qkv_weight.shape[1], proj_weight.shape[1]
     gain_cols, height = norm_gains.shape[1], -(-max(n_up + 2, n_qkv + n_proj) // 8) * 8
-    gain_rows = jnp.pad(norm_gains, ((0, height - n_up - 2), (0, features - gain_cols)))
+    gain_spot = lax.axis_index("lon") * gain_cols
+    gain_rows = lax.dynamic_update_slice(
+        jnp.zeros((height - n_up, features), BF16), norm_gains, (jnp.int32(0), gain_spot)
+    )
     a_part = jnp.stack(
         [
             jnp.concatenate([up_weight.T, gain_rows]),
@@ -344,9 +396,7 @@
         ]
     )
     d_part = down_weight.reshape(2, -1, down_weight.shape[1]).transpose(0, 2, 1)
-    b_part = jnp.concatenate(
-        [lax.dynamic_index_in_dim(bias_table, types[i], 0, keepdims=False) for i in range(positions)], axis=0
-    )
+    b_part = pick_rows(types, bias_table)
     both = jnp.roll(jnp.stack([inputs, cotangent]), -level_shift, axis=1)
     rim_lat = both[:, :, :row_half, col_half:]
     rim_lon = both[:, :, row_half:, :col_half]
@@ -360,32 +410,15 @@
         [dma((3, nlon // 2))] * 4 + [dma((2, nlon))] * 2 + [dma((3,))] * 2,
         (a_part, d_part, b_part, *flat),
     )
-    up_t = a_all[:, 0, :n_up].reshape(-1, features)
-    qkv_t = a_all[:, 1, :n_qkv].reshape(-1, features)
-    proj_t = a_all[:, 1, n_qkv : n_qkv + n_proj].reshape(-1, features)
-    gains = a_all[:, 0, n_up : n_up + 2, :gain_cols].transpose(1, 0, 2).reshape(2, features)
-    down_t = d_all.transpose(0, 2, 1, 3).reshape(features, -1)
     bias = b_all.transpose(1, 0, 2).reshape(positions, head_count, WIN, WIN)
     top = jnp.concatenate([both[:, :, row_half:, col_half:], r_lon.reshape(rim_lon.shape)], axis=3)
     bottom = jnp.concatenate([r_lat.reshape(rim_lat.shape), r_diag.reshape(rim_diag.shape)], axis=3)
     shifted = jnp.concatenate([top, bottom], axis=2)
     labels = region.reshape(level_windows, WPL, row_windows, WLAT).transpose(0, 2, 1, 3)
     labels = jnp.broadcast_to(labels[..., None], labels.shape + (WLON,)).reshape(positions, WIN)
-    d_cells, g_qkv_t, g_proj_t, g_up_t, g_down_t, g_gains, table = block_grads(
-        to_windows(shifted[0]), to_windows(shifted[1]), qkv_t, proj_t, up_t, down_t, gains, bias, labels
-    )
-    g_gain_rows = g_gains.reshape(2, nlon, gain_cols).transpose(1, 0, 2)
-    g_gain_rows = jnp.pad(g_gain_rows, ((0, 0), (0, height - n_up - 2), (0, features - gain_cols)))
-    g_up_t, g_qkv_t, g_proj_t = (g.reshape(nlon, -1, features) for g in (g_up_t, g_qkv_t, g_proj_t))
-    ga = jnp.stack(
-        [
-            jnp.concatenate([g_up_t, g_gain_rows], axis=1),
-            jnp.pad(
-                jnp.concatenate([g_qkv_t, g_proj_t], axis=1), ((0, 0), (0, height - n_qkv - n_proj), (0, 0))
-            ),
-        ]
-    ).astype(BF16)
-    gd = g_down_t.reshape(nlon, -1, 2, g_down_t.shape[1] // 2).transpose(2, 0, 1, 3).astype(BF16)
+    d_cells, ga, gd, table = block_grads(
+        to_windows(shifted[0]), to_windows(shifted[1]), a_all, d_all, (n_up, n_qkv, n_proj), bias, labels
+    )
     gt = table.astype(BF16).reshape(positions * head_count, nlon, part).transpose(1, 0, 2)
     onehot = (all_types[:, None, :] == jnp.arange(type_count, dtype=jnp.int32)[None, :, None]).astype(BF16)
     kron = jnp.einsum("lyp,gh->lygph", onehot, jnp.eye(head_count, dtype=BF16)).reshape(
@@ -420,7 +453,7 @@
         a_sum[1, n_qkv : n_qkv + n_proj].T,
         a_sum[0, :n_up].T,
         d_sum.transpose(0, 2, 1).reshape(down_weight.shape),
-        a_sum[0, n_up : n_up + 2, :gain_cols],
+        lax.dynamic_slice(a_sum[0, n_up : n_up + 2], (jnp.int32(0), gain_spot), (2, gain_cols)),
         t_sum.reshape(type_count, head_count, part),
     )
 

time: 131 us -> 128 us (0.977)
  between operations: 7.1 us -> 1.03 us
  Pallas kernels: 92.5 us -> 94.4 us
  local copies, waits for them, and re-layouts: 28.6 us -> 30.5 us
    unnamed x59 -> x55, local copies, waits for them, and re-layouts: 10.7 us -> 15 us
    pallas_call x1 -> x2, Pallas kernels: 19 us -> 21 us  [the longest x1 19.2 us: block_grads(): pl.pallas_call(functools.partial(window_kernel, *cuts), out_shape=[jax.Sh...]
    dynamic_update_slice x0 -> x1, local copies, waits for them, and re-layouts: none -> 1.49 us  [shards(): lax.dynamic_update_slice(jnp.zeros((height - n_up, features), BF16), norm...]
    another operation x9 -> x2, other arithmetic: 1.53 us -> 0.08 us
where the time goes in v4:
time: 128 us
  Pallas kernels  94.4 us (74%)
  local copies, waits for them, and re-layouts  30.5 us (24%)
  other arithmetic  1.79 us (1%)
    pallas_call x2, Pallas kernels, comm_call(): pl.pallas_call(kernel, out_shape=[jax.ShapeDtypeStruct(*o) for o in outs]...  73.4 us
    pallas_call x1, Pallas kernels, block_grads(): pl.pallas_call(functools.partial(window_kernel, *cuts), out_shape=[jax.Sh...  19.2 us
    unnamed x55, local copies, waits for them, and re-layouts  15 us
    reshape x2, local copies, waits for them, and re-layouts, shards(): table.astype(BF16).reshape(positions * head_count, nlon, part)  3.6 us

profile of v4, /device:TPU:0, one launch (start us, length us, event | category | flops | bytes accessed | tf_op | source)
XLA Modules:
  0.0 127.8 jit_solution(12924115435245838620)
XLA Ops:
  0.6 1.5 %dynamic_update_slice.3 = bf16[8,192]{1,0:T(8,128)(2,1)S(1)} dynamic-update-slice(bf16[8,192]{1,0:T(8,128)(2,1)S(1)} %broadcast_in_dim.15, bf16[2,24]{1,0:T(2,128)(2,1)} %param.16, s32[]{:T(128)} %constant.18.clone.1, s32[]{:T(128)S(6)} %select_n.8) | dynamic-update-slice | bytes 196 | tf_op jit(solution)/shard_map/dynamic_update_slice | solution.py:387
  2.1 0.9 copy.37
  3.0 0.8 fusion.8
  3.9 1.2 copy_bitcast_fusion.1
  6.1 0.7 dynamic-slice_reduce_fusion.types
  6.8 1.0 copy.39.table
  7.8 1.8 %shard_map.153.b = bf16[24,2592]{1,0:T(8,128)(2,1)} custom-call(s32[4]{0:T(128)} %dynamic-slice_reduce_fusion.types, bf16[16,6,2592]{2,1,0:T(8,128)(2,1)} %copy.39.table), custom_call_target="tpu_custom_call" | custom-call | tf_op jit(solution)/shard_map/pallas_call | solution.py:240
  9.6 0.9 copy-done.2
  10.5 32.8 %shard_map.154 = (bf16[8,2,104,192]{3,2,1,0:T(8,128)(2,1)S(1)}, bf16[8,2,24,384]{3,2,1,0:T(8,128)(2,1)S(1)}, bf16[8,24,2592]{2,1,0:T(8,128)(2,1)S(1)}, bf16[288,...) custom-call(bf16[2,104,192]{2,1,0:T(8,128)(2,1)S(1)} %pad_maximum_fusion.5.a, ...), custom_call_target="tpu_custom_call" | custom-call | tf_op jit(solution)/shard_map/pallas_call | solution.py:197
  43.3 0.9 copy-done
  44.1 0.7 copy-done.5
  45.9 2.3 %reshape.96.bias = bf16[4,6,144,144]{3,2,1,0:T(8,128)(2,1)} reshape(bf16[24,8,2592]{2,1,0:T(8,128)(2,1)S(1)} %copy.40) | data formatting | bytes 1990656 | tf_op jit(solution)/shard_map/reshape | solution.py:413
  48.5 1.1 copy-done.1
  49.6 1.0 copy-done.6
  50.6 19.2 %shard_map.155 = (bf16[4,144,192]{2,1,0:T(8,128)(2,1)S(1)}, bf16[2,8,104,192]{3,2,1,0:T(8,128)(2,1)S(1)}, bf16[2,8,24,384]{3,2,1,0:T(8,128)(2,1)S(1)}, bf16[4,6,144,144]{3,2,1,0:T(8,128)(2,1)S(1)}) custom-call(bf16[4,144,192]{2,1,0:T(8,128)(2,1)S(1)} %reshape_reshape_transpose_reshape_squeeze.6.cells, ...), custom_call_target="tpu_custom_call" | custom-call | tf_op jit(solution)/shard_map/pallas_call | solution.py:358
  69.8 0.7 copy-done.3
  70.5 0.7 copy-done.8
  71.2 2.2 %reshape.97 = bf16[24,8,2592]{2,1,0:T(8,128)(2,1)} reshape(bf16[4,6,144,144]{3,2,1,0:T(8,128)(2,1)S(1)} %get-tuple-element.31) | data formatting | bytes 1990656 | tf_op jit(solution)/shard_map/reshape | solution.py:422
  73.5 1.4 %copy.56 = bf16[24,8,2592]{2,0,1:T(8,128)(2,1)S(1)} copy(bf16[24,8,2592]{2,1,0:T(8,128)(2,1)} %reshape.97) | data formatting | bytes 1990656 | tf_op jit(solution)/shard_map/reshape | solution.py:422
  74.9 0.7 fusion.13
  75.8 0.7 reshape.102.h_diag
  77.2 0.9 copy-done.7
  78.1 40.7 %shard_map.156 = (f32[2,104,192]{2,1,0:T(8,128)S(1)}, f32[2,24,384]{2,1,0:T(8,128)S(1)}, f32[96,2592]{1,0:T(8,128)S(1)}, bf16[144,192]{1,0:T(8,128)(2,1)S(1)}, b...) custom-call(bf16[2,8,104,192]{3,2,1,0:T(8,128)(2,1)S(1)} %get-tuple-element.29.a, ...), custom_call_target="tpu_custom_call" | custom-call | tf_op jit(solution)/shard_map/pallas_call | solution.py:197
  118.8 0.7 copy-done.10
  120.1 0.6 copy-done.14
  120.7 0.6 copy-done.16
  122.2 1.1 copy.49
  123.6 0.9 copy.47
  124.5 0.7 copy.48
  125.3 0.6 copy.51
  125.9 0.6 slice_bitcast_fusion.1
  127.2 0.6 dynamic-slice_bitcast_fusion
  (76 shorter events, 5.5 us)
Async XLA Ops:
  5.4 0.7 copy-start.23
  5.4 1.4 %copy-start.20 = (bf16[16,6,2592]{2,0,1:T(8,128)(2,1)S(1)}, bf16[16,6,2592]{2,0,1:T(8,128)(2,1)}, u32[]{:S(2)}) copy-start(bf16[16,6,2592]{2,0,1:T(8,128)(2,1)} %param.17) | copy-start | bytes 1492996
  5.6 4.0 %copy-start.22 = (bf16[768,24]{0,1:T(8,128)(2,1)S(1)}, bf16[768,24]{0,1:T(8,128)(2,1)}, u32[]{:S(2)}) copy-start(bf16[768,24]{0,1:T(8,128)(2,1)} %param.15) | copy-start | bytes 110596
  9.6 0.9 copy-start.2
  43.2 0.9 copy-start
  44.1 0.7 copy-start.5
  45.9 2.3 %copy-start.24 = (s32[8,6]{1,0:T(8,128)S(1)}, s32[8,6]{1,0:T(8,128)}, u32[]{:S(2)}) copy-start(s32[8,6]{1,0:T(8,128)} %param.19) | copy-start | bytes 580
  48.4 1.2 copy-start.1
  49.6 1.0 copy-start.6
  69.8 0.7 copy-start.3
  70.5 0.7 copy-start.8
  73.5 1.4 %copy-start.9 = (bf16[4,144,192]{2,1,0:T(8,128)(2,1)S(1)}, bf16[4,144,192]{2,1,0:T(8,128)(2,1)}, u32[]{:S(2)}) copy-start(bf16[4,144,192]{2,1,0:T(8,128)(2,1)} %copy-done.8) | copy-start | bytes 663556
  74.8 2.4 %copy-start.4 = (bf16[2,8,24,384]{3,2,1,0:T(8,128)(2,1)S(1)}, bf16[2,8,24,384]{3,2,1,0:T(8,128)(2,1)}, u32[]{:S(2)}) copy-start(bf16[2,8,24,384]{3,2,1,0:T(8,128)(2,1)} %copy-done.3) | copy-start | bytes 884740
  77.2 0.9 copy-start.7
  118.8 0.7 copy-start.10
  119.5 0.6 copy-start.12
  120.1 0.6 copy-start.14
  120.7 0.6 copy-start.16
  121.4 0.6 copy-start.18
  122.1 1.2 copy-start.19
  122.1 1.2 copy-start.17
  122.2 1.3 copy-start.15
  122.2 1.3 %copy-start.21 = (bf16[8,3,6,192]{3,2,1,0:T(8,128)(2,1)S(1)}, bf16[8,3,6,192]{3,2,1,0:T(8,128)(2,1)}, u32[]{:S(2)}) copy-start(bf16[8,3,6,192]{3,2,1,0:T(8,128)(2,1)} %get-tuple-element.60) | copy-start | bytes 165892
  123.3 1.2 copy-start.11
  123.3 1.9 %copy-start.13 = (f32[2,24,384]{2,1,0:T(8,128)S(1)}, f32[2,24,384]{2,1,0:T(8,128)}, u32[]{:S(2)}) copy-start(f32[2,24,384]{2,1,0:T(8,128)} %copy-done.12) | copy-start | bytes 221188

commit v5 on v4

--- a/solution.py
+++ b/solution.py
@@ -384,9 +384,9 @@
     n_up, n_qkv, n_proj = up_weight.shape[1], qkv_weight.shape[1], proj_weight.shape[1]
     gain_cols, height = norm_gains.shape[1], -(-max(n_up + 2, n_qkv + n_proj) // 8) * 8
     gain_spot = lax.axis_index("lon") * gain_cols
-    gain_rows = lax.dynamic_update_slice(
-        jnp.zeros((height - n_up, features), BF16), norm_gains, (jnp.int32(0), gain_spot)
-    )
+    own_lane = jnp.arange(features, dtype=jnp.int32) // gain_cols == lax.axis_index("lon")
+    gain_rows = jnp.where(own_lane, jnp.tile(norm_gains, (1, nlon)), jnp.zeros((), BF16))
+    gain_rows = jnp.pad(gain_rows, ((0, height - n_up - 2), (0, 0)))
     a_part = jnp.stack(
         [
             jnp.concatenate([up_weight.T, gain_rows]),

time: 128 us -> 125 us (0.977)
  local copies, waits for them, and re-layouts: 30.5 us -> 28.3 us
    dynamic_update_slice x1 -> x0, local copies, waits for them, and re-layouts: 1.49 us -> none  [shards(): lax.dynamic_update_slice(jnp.zeros((height - n_up, features), BF16), norm...]
    unnamed x55 -> x63, local copies, waits for them, and re-layouts: 15 us -> 14.2 us
where the time goes in v5:
time: 125 us
  Pallas kernels  94.2 us (75%)
  local copies, waits for them, and re-layouts  28.3 us (23%)
    pallas_call x2, Pallas kernels, comm_call(): pl.pallas_call(kernel, out_shape=[jax.ShapeDtypeStruct(*o) for o in outs]...  73.2 us
    pallas_call x1, Pallas kernels, block_grads(): pl.pallas_call(functools.partial(window_kernel, *cuts), out_shape=[jax.Sh...  19.2 us
    unnamed x63, local copies, waits for them, and re-layouts  14.2 us
    reshape x2, local copies, waits for them, and re-layouts, shards(): table.astype(BF16).reshape(positions * head_count, nlon, part)  3.6 us

profile of v5, /device:TPU:0, one launch (start us, length us, event | category | flops | bytes accessed | tf_op | source)
XLA Modules:
  0.0 124.7 jit_solution(17269702392092154490)
XLA Ops:
  0.6 1.2 copy_bitcast_fusion.1
  2.9 0.7 dynamic-slice_reduce_fusion.types
  3.5 1.0 copy.39.table
  4.5 1.8 %shard_map.153.b = bf16[24,2592]{1,0:T(8,128)(2,1)} custom-call(s32[4]{0:T(128)} %dynamic-slice_reduce_fusion.types, bf16[16,6,2592]{2,1,0:T(8,128)(2,1)} %copy.39.table), custom_call_target="tpu_custom_call" | custom-call | tf_op jit(solution)/shard_map/pallas_call | solution.py:240
  6.7 0.9 copy-done.2
  7.6 32.6 %shard_map.154 = (bf16[8,2,104,192]{3,2,1,0:T(8,128)(2,1)S(1)}, bf16[8,2,24,384]{3,2,1,0:T(8,128)(2,1)S(1)}, bf16[8,24,2592]{2,1,0:T(8,128)(2,1)S(1)}, bf16[288,...) custom-call(bf16[2,104,192]{2,1,0:T(8,128)(2,1)S(1)} %pad_maximum_fusion.5.a, ...), custom_call_target="tpu_custom_call" | custom-call | tf_op jit(solution)/shard_map/pallas_call | solution.py:197
  40.2 0.9 copy-done
  41.1 0.7 copy-done.5
  42.8 2.3 %reshape.100.bias = bf16[4,6,144,144]{3,2,1,0:T(8,128)(2,1)} reshape(bf16[24,8,2592]{2,1,0:T(8,128)(2,1)S(1)} %copy.40) | data formatting | bytes 1990656 | tf_op jit(solution)/shard_map/reshape | solution.py:413
  45.4 1.1 copy-done.1
  46.5 1.0 copy-done.6
  47.5 19.2 %shard_map.155 = (bf16[4,144,192]{2,1,0:T(8,128)(2,1)S(1)}, bf16[2,8,104,192]{3,2,1,0:T(8,128)(2,1)S(1)}, bf16[2,8,24,384]{3,2,1,0:T(8,128)(2,1)S(1)}, bf16[4,6,144,144]{3,2,1,0:T(8,128)(2,1)S(1)}) custom-call(bf16[4,144,192]{2,1,0:T(8,128)(2,1)S(1)} %reshape_reshape_transpose_reshape_squeeze.6.cells, ...), custom_call_target="tpu_custom_call" | custom-call | tf_op jit(solution)/shard_map/pallas_call | solution.py:358
  66.7 0.7 copy-done.3
  67.4 0.7 copy-done.8
  68.1 2.2 %reshape.101 = bf16[24,8,2592]{2,1,0:T(8,128)(2,1)} reshape(bf16[4,6,144,144]{3,2,1,0:T(8,128)(2,1)S(1)} %get-tuple-element.31) | data formatting | bytes 1990656 | tf_op jit(solution)/shard_map/reshape | solution.py:422
  70.4 1.4 %copy.56 = bf16[24,8,2592]{2,0,1:T(8,128)(2,1)S(1)} copy(bf16[24,8,2592]{2,1,0:T(8,128)(2,1)} %reshape.101) | data formatting | bytes 1990656 | tf_op jit(solution)/shard_map/reshape | solution.py:422
  71.9 0.7 fusion.17
  72.7 0.7 reshape.106.h_diag
  74.2 0.9 copy-done.7
  75.0 40.6 %shard_map.156 = (f32[2,104,192]{2,1,0:T(8,128)S(1)}, f32[2,24,384]{2,1,0:T(8,128)S(1)}, f32[96,2592]{1,0:T(8,128)S(1)}, bf16[144,192]{1,0:T(8,128)(2,1)S(1)}, b...) custom-call(bf16[2,8,104,192]{3,2,1,0:T(8,128)(2,1)S(1)} %get-tuple-element.29.a, ...), custom_call_target="tpu_custom_call" | custom-call | tf_op jit(solution)/shard_map/pallas_call | solution.py:197
  115.7 0.7 copy-done.10
  116.3 0.6 copy-done.12
  117.0 0.6 copy-done.14
  117.6 0.6 copy-done.16
  118.2 0.6 copy-done.18
  119.0 1.1 copy.49
  120.5 0.9 copy.47
  121.4 0.7 copy.48
  122.1 0.6 copy.51
  122.8 0.6 slice_bitcast_fusion.1
  123.4 0.6 slice_bitcast_fusion.2
  124.0 0.6 dynamic-slice_bitcast_fusion
  (86 shorter events, 3.8 us)
Async XLA Ops:
  2.2 0.7 copy-start.26
  2.2 1.4 %copy-start.20 = (bf16[16,6,2592]{2,0,1:T(8,128)(2,1)S(1)}, bf16[16,6,2592]{2,0,1:T(8,128)(2,1)}, u32[]{:S(2)}) copy-start(bf16[16,6,2592]{2,0,1:T(8,128)(2,1)} %param.17) | copy-start | bytes 1492996
  2.3 4.0 %copy-start.28 = (bf16[2,24]{1,0:T(2,128)(2,1)S(1)}, bf16[2,24]{1,0:T(2,128)(2,1)}, u32[]{:S(2)}) copy-start(bf16[2,24]{1,0:T(2,128)(2,1)} %param.16) | copy-start | bytes 292
  2.3 4.1 %copy-start.22 = (bf16[192,96]{1,0:T(8,128)(2,1)S(1)}, bf16[192,96]{1,0:T(8,128)(2,1)}, u32[]{:S(2)}) copy-start(bf16[192,96]{1,0:T(8,128)(2,1)} %param.14) | copy-start | bytes 110596
  2.4 4.2 %copy-start.23 = (bf16[192,72]{0,1:T(8,128)(2,1)S(1)}, bf16[192,72]{0,1:T(8,128)(2,1)}, u32[]{:S(2)}) copy-start(bf16[192,72]{0,1:T(8,128)(2,1)} %param.12) | copy-start | bytes 82948
  2.4 4.2 %copy-start.25 = (bf16[192,24]{0,1:T(8,128)(2,1)S(1)}, bf16[192,24]{0,1:T(8,128)(2,1)}, u32[]{:S(2)}) copy-start(bf16[192,24]{0,1:T(8,128)(2,1)} %param.13) | copy-start | bytes 27652
  2.5 4.2 %copy-start.24 = (bf16[768,24]{0,1:T(8,128)(2,1)S(1)}, bf16[768,24]{0,1:T(8,128)(2,1)}, u32[]{:S(2)}) copy-start(bf16[768,24]{0,1:T(8,128)(2,1)} %param.15) | copy-start | bytes 110596
  6.7 0.9 copy-start.2
  40.2 0.9 copy-start
  41.1 0.7 copy-start.5
  42.8 2.3 %copy-start.27 = (s32[8,6]{1,0:T(8,128)S(1)}, s32[8,6]{1,0:T(8,128)}, u32[]{:S(2)}) copy-start(s32[8,6]{1,0:T(8,128)} %param.19) | copy-start | bytes 580
  45.3 1.2 copy-start.1
  46.5 1.0 copy-start.6
  66.7 0.7 copy-start.3
  67.4 0.7 copy-start.8
  70.4 1.4 %copy-start.9 = (bf16[4,144,192]{2,1,0:T(8,128)(2,1)S(1)}, bf16[4,144,192]{2,1,0:T(8,128)(2,1)}, u32[]{:S(2)}) copy-start(bf16[4,144,192]{2,1,0:T(8,128)(2,1)} %copy-done.8) | copy-start | bytes 663556
  71.7 2.4 %copy-start.4 = (bf16[2,8,24,384]{3,2,1,0:T(8,128)(2,1)S(1)}, bf16[2,8,24,384]{3,2,1,0:T(8,128)(2,1)}, u32[]{:S(2)}) copy-start(bf16[2,8,24,384]{3,2,1,0:T(8,128)(2,1)} %copy-done.3) | copy-start | bytes 884740
  74.1 0.9 copy-start.7
  115.7 0.7 copy-start.10
  116.3 0.6 copy-start.12
  117.0 0.6 copy-start.14
  117.6 0.6 copy-start.16
  118.2 0.6 copy-start.18
  119.0 1.2 copy-start.19
  119.0 1.2 copy-start.17
  119.0 1.3 %copy-start.15 = (bf16[144,192]{1,0:T(8,128)(2,1)S(1)}, bf16[144,192]{1,0:T(8,128)(2,1)}, u32[]{:S(2)}) copy-start(bf16[144,192]{1,0:T(8,128)(2,1)} %copy-done.14) | copy-start | bytes 165892
  119.0 1.3 %copy-start.21 = (bf16[8,3,6,192]{3,2,1,0:T(8,128)(2,1)S(1)}, bf16[8,3,6,192]{3,2,1,0:T(8,128)(2,1)}, u32[]{:S(2)}) copy-start(bf16[8,3,6,192]{3,2,1,0:T(8,128)(2,1)} %get-tuple-element.60) | copy-start | bytes 165892
  120.2 1.2 copy-start.11
  120.2 1.9 %copy-start.13 = (f32[2,24,384]{2,1,0:T(8,128)S(1)}, f32[2,24,384]{2,1,0:T(8,128)}, u32[]{:S(2)}) copy-start(f32[2,24,384]{2,1,0:T(8,128)} %copy-done.12) | copy-start | bytes 221188
